TPU v7x, 256 devices: a whole 4x4x8 slice. The times are simulated.
256 devices in a mesh: wide: 32 (over z_hi, y, x), narrow: 8 (over z_lo, core).
Axes of the slice: x: 4, y: 4, z: 8 (z_hi: 2, z_lo: 4; z = z_hi * 4 + z_lo), core: 2. Of those that a mesh axis runs over, the one named last changes fastest.
Arguments:
- tile_pool: bfloat16 [32, 1024, 768], P('wide', 'narrow'), may hold values from -96 to 96
- batch_index: int32 [32, 2048], P('wide', 'narrow'), may hold values from 0 to 127
- pair_label: int32 [32, 2048], P('wide', 'narrow'), may hold values from 0 to 255, as said below
- w_first: bfloat16 [768, 2048], P('narrow'), may hold values from -0.375 to 0.375
- w_second: bfloat16 [2048, 2048], P('narrow'), may hold values from -0.375 to 0.375
- m_first: bfloat16 [32, 768, 2048], P('wide', 'narrow'), may hold values from -0.01275776 to 0.01275776
- m_second: bfloat16 [32, 2048, 2048], P('wide', 'narrow'), may hold values from -0.0078125 to 0.0078125
- v_first: bfloat16 [32, 768, 2048], P('wide', 'narrow'), may hold values from 0.0005086263 to 0.025431315
- v_second: bfloat16 [32, 2048, 2048], P('wide', 'narrow'), may hold values from 0.00019073486 to 0.009536743
- mom_first: bfloat16 [768, 2048], P('narrow'), may hold values from -0.1796875 to 0.1796875
- mom_second: bfloat16 [2048, 2048], P('narrow'), may hold values from -0.1796875 to 0.1796875
Outputs:
- new_first: bfloat16 [768, 2048], P('narrow')
- new_second: bfloat16 [2048, 2048], P('narrow')
- mom_out_first: bfloat16 [768, 2048], P('narrow')
- mom_out_second: bfloat16 [2048, 2048], P('narrow')
Inputs may be any that keep to these rules, and one draw needn't show every extreme that they name: `batch_index`: indices count within the pool of the same site and shard. `pair_label`: each row's partner is another row of the same site and shard, counted within that shard's 256 rows, and names the row back.
All inputs are finite; a program needn't handle non-finite values.
Results may differ from a plain program's by a relative error of at most 0.0075.
Values may be sent and summed in bfloat16 or wider, within the bound.
A program may use at most 128 MiB of HBM per device.

v0:
```python
import math

import jax
import jax.numpy as jnp
from jax import lax
from jax.sharding import PartitionSpec as P

PIX = 768
MID = 2048
OUT = 2048


logit_scale = 1.0 / 0.07
rate_inner = 0.2
weight_decay = 0.1
beta_first = 0.9
beta_second = 0.95
adam_eps = 1e-08
rate_outer = 0.7
momentum_coef = 0.9


def adam_delta(grads, first_moment, second_moment, weights):
    moment_one = beta_first * first_moment.astype(jnp.float32) + (1.0 - beta_first) * grads
    moment_two = (
        beta_second * second_moment.astype(jnp.float32) + (1.0 - beta_second) * grads * grads
    )
    return rate_inner * (
        moment_one / (jnp.sqrt(moment_two) + adam_eps) + weight_decay * weights.astype(jnp.float32)
    )


def outer_update(delta, momentum, weights):
    velocity = momentum_coef * momentum.astype(jnp.float32) + delta
    updated = weights.astype(jnp.float32) - rate_outer * (delta + momentum_coef * velocity)
    return (updated.astype(jnp.bfloat16), velocity.astype(jnp.bfloat16))


def embed_gradient(embedded, partner):
    inverse = lax.rsqrt(jnp.sum(embedded * embedded, axis=1, keepdims=True) + OUT * 1e-06)
    unit_rows = embedded * inverse
    unit_half = unit_rows.astype(jnp.bfloat16)
    scores = logit_scale * jnp.dot(unit_half, unit_half.T, preferred_element_type=jnp.float32)
    positions = jnp.arange(embedded.shape[0], dtype=jnp.int32)
    diagonal = positions[:, None] == positions[None, :]
    scores = jnp.where(diagonal, -1e30, scores)
    highest = jnp.max(scores, axis=1, keepdims=True)
    powers = jnp.exp(scores - highest)
    softmax_rows = powers / jnp.sum(powers, axis=1, keepdims=True)
    target = (partner[:, None] == positions[None, :]).astype(jnp.float32)
    score_grad = softmax_rows - target
    paired = (score_grad + score_grad.T).astype(jnp.bfloat16)
    unit_grad = logit_scale * jnp.dot(paired, unit_half, preferred_element_type=jnp.float32)
    embed_grad = inverse * (
        unit_grad - unit_rows * jnp.sum(unit_rows * unit_grad, axis=1, keepdims=True)
    )
    return embed_grad.astype(jnp.bfloat16)


def shards(
    tile_pool,
    batch_index,
    pair_label,
    w_first,
    w_second,
    m_first,
    m_second,
    v_first,
    v_second,
    mom_first,
    mom_second,
):
    inputs = jnp.take(tile_pool[0], batch_index[0], axis=0)
    partner = pair_label[0]
    scale_one = 1.0 / math.sqrt(PIX)
    scale_two = 1.0 / math.sqrt(MID)
    hidden = (
        jnp.dot(
            inputs,
            lax.all_gather(w_first, "narrow", axis=0, tiled=True),
            preferred_element_type=jnp.float32,
        )
        * scale_one
    )
    active_full, gelu_back = jax.vjp(jax.nn.gelu, hidden)
    active = active_full.astype(jnp.bfloat16)
    second_whole = lax.all_gather(w_second, "narrow", axis=0, tiled=True)
    embedded = jnp.dot(active, second_whole, preferred_element_type=jnp.float32) * scale_two
    embed_half = embed_gradient(embedded, partner)
    block = active
    grad_second = lax.psum_scatter(
        (scale_two * jnp.dot(block.T, embed_half, preferred_element_type=jnp.float32)).astype(
            jnp.bfloat16
        ),
        "narrow",
        scatter_dimension=0,
        tiled=True,
    ).astype(jnp.float32)
    delta_second = adam_delta(grad_second, m_second[0], v_second[0], w_second)
    active_grad = scale_two * jnp.dot(
        embed_half, second_whole.T, preferred_element_type=jnp.float32
    )
    hidden_half = gelu_back(active_grad)[0].astype(jnp.bfloat16)
    block = inputs
    grad_first = lax.psum_scatter(
        (scale_one * jnp.dot(block.T, hidden_half, preferred_element_type=jnp.float32)).astype(
            jnp.bfloat16
        ),
        "narrow",
        scatter_dimension=0,
        tiled=True,
    ).astype(jnp.float32)
    delta_first = adam_delta(grad_first, m_first[0], v_first[0], w_first)
    sites_count = lax.axis_size("wide")
    summed_first, summed_second = lax.psum((delta_first, delta_second), "wide")
    new_first, velocity_first = outer_update(summed_first / sites_count, mom_first, w_first)
    new_second, velocity_second = outer_update(summed_second / sites_count, mom_second, w_second)
    return (new_first, new_second, velocity_first, velocity_second)


def solution(mesh):
    return jax.shard_map(
        shards,
        mesh=mesh,
        in_specs=(
            P("wide", "narrow", None),
            P("wide", "narrow"),
            P("wide", "narrow"),
            P("narrow", None),
            P("narrow", None),
            P("wide", "narrow", None),
            P("wide", "narrow", None),
            P("wide", "narrow", None),
            P("wide", "narrow", None),
            P("narrow", None),
            P("narrow", None),
        ),
        out_specs=(P("narrow", None), P("narrow", None), P("narrow", None), P("narrow", None)),
        check_vma=False,
    )
```

profile of v0, /device:TPU:64, one launch (start us, length us, event | category | flops | bytes accessed | tf_op | source)
XLA Modules:
  0.0 765.5 jit_solution(353269186238694735)
XLA Ops:
  7.2 0.0 copy-start
  7.2 0.0 all-gather.3.cloned.1.call-start
  7.2 0.7 all-gather.3.cloned.1.call-update
  7.9 0.0 copy-start.11
  7.9 0.0 all-gather.5.cloned.1.call-start
  8.0 0.7 all-gather.5.cloned.1.call-update
  8.7 0.0 reduce-scatter.3.cloned.1.call-start
  8.7 0.7 compare_select_fusion
  9.4 0.0 copy-done
  9.4 1.2 gather_fusion
  10.6 0.0 copy-done.11
  10.6 42.6 %all-gather.3.cloned.1.call-done = bf16[768,2048]{1,0:T(8,128)(2,1)} async-done(((bf16[96,2048]{1,0:T(8,128)(2,1)}), bf16[768,2048]{1,0:T(8,128)(2,1)}) %all-gather.3.cloned.1.call-update) | async-done | bytes 3145744 | tf_op jit(solution)/shard_map/all_gather | solution.py:80
  53.2 4.4 convolution_multiply_fusion.1
  57.6 91.0 %all-gather.5.cloned.1.call-done = bf16[2048,2048]{1,0:T(8,128)(2,1)} async-done(((bf16[256,2048]{1,0:T(8,128)(2,1)}), bf16[2048,2048]{1,0:T(8,128)(2,1)}) %all-gather.5.cloned.1.call-update) | async-done | bytes 8388624 | tf_op jit(solution)/shard_map/all_gather | solution.py:87
  148.6 6.7 multiply_reduce_fusion.1
  155.3 0.0 copy-start.12
  155.3 0.6 convolution_multiply_fusion.3
  155.9 0.1 copy.16
  156.0 0.1 fusion.39
  156.1 0.2 fusion.40
  156.3 0.0 copy-done.12
  156.4 0.8 multiply_reduce_fusion
  157.1 1.5 multiply_convert_fusion.2
  158.6 10.2 %multiply_convert_fusion.1 = bf16[768,2048]{1,0:T(8,128)(2,1)} fusion(f32[256,2048]{1,0:T(8,128)} %convolution_multiply_fusion.1, bf16[256,2048]{1,0:T(8,128)(2,1)} %multiply_convert_fusion.2, bf16[2048,2048]{1,0:T(8,128)(2,1)} %all-gather.5.cloned.1.call-done, bf16[256,768]{1,0:T(8,128)(2,1)S(1)} %gather_fusion, pred[256]{0:T(512)(128)(4,1)S(1)} %compare_and_fusion), kind=kOutput, calls=%fused_computation.2 | convolution fusion | flops 2967142400 | bytes 15073536 | tf_op jit(solution)/shard_map/dot_general | solution.py:106
  168.8 0.0 reduce-scatter.3.cloned.1.call-update
  168.8 0.2 reduce-scatter.5.cloned.1.call-start
  169.1 1.3 copy-done.3
  170.4 0.3 copy-done.7
  170.7 6.2 multiply_convert_fusion
  177.0 0.0 reduce-scatter.5.cloned.1.call-update
  177.0 0.0 copy-start.1
  177.0 0.0 copy-start.5
  177.0 0.0 all-reduce.3.cloned.1.call-start
  177.1 35.6 %reduce-scatter.3.cloned.1.call-done = bf16[96,2048]{1,0:T(8,128)(2,1)} async-done(((bf16[768,2048]{1,0:T(8,128)(2,1)}), bf16[96,2048]{1,0:T(8,128)(2,1)}) %reduce-scatter.3.cloned.1.call-update) | async-done | bytes 393232 | tf_op jit(solution)/shard_map/reduce_scatter | solution.py:105
  212.7 0.0 copy-done.2
  212.7 0.0 copy-done.8
  212.7 0.0 copy-done.9
  212.7 2.5 fusion.24
  215.2 95.3 %reduce-scatter.5.cloned.1.call-done = bf16[256,2048]{1,0:T(8,128)(2,1)} async-done(((bf16[2048,2048]{1,0:T(8,128)(2,1)}), bf16[256,2048]{1,0:T(8,128)(2,1)}) %reduce-scatter.5.cloned.1.call-update) | async-done | bytes 1048592 | tf_op jit(solution)/shard_map/reduce_scatter | solution.py:91
  310.5 0.0 copy-done.1
  310.5 0.0 copy-done.5
  310.5 4.5 fusion.1
  315.0 0.0 all-reduce.3.cloned.1.call-update
  315.0 439.4 %all-reduce.3.cloned.1.call-done = (f32[96,2048]{1,0:T(8,128)}, f32[256,2048]{1,0:T(8,128)}) async-done(((f32[96,2048]{1,0:T(8,128)}, f32[256,2048]{1,0:T(8,128)}), (f32[96,2048]{1,0:T(8,128)}, f32[256,2048]{1,0:T(8,128)})) %all-reduce.3.cloned.1.call-update) | async-done | bytes 2883600 | tf_op jit(solution)/shard_map/psum | solution.py:115
  754.5 0.0 copy-done.10
  754.5 2.4 fusion.31
  756.9 0.0 copy-done.6
  756.9 2.0 fusion.15
  (12 shorter events, 0.0 us)
Async XLA Ops:
  7.2 2.2 copy-start
  7.2 46.0 %all-gather.3.cloned.1.call-start = ((), (), s32[]{:S(2)}) async-start(), calls=%async_computation.2 | async-start | bytes 3538944 | tf_op jit(solution)/shard_map/all_gather | solution.py:80
  7.9 2.7 copy-start.11
  7.9 140.7 %all-gather.5.cloned.1.call-start = ((), (), s32[]{:S(2)}) async-start(), calls=%async_computation.3 | async-start | bytes 9437184 | tf_op jit(solution)/shard_map/all_gather | solution.py:87
  8.7 204.0 %reduce-scatter.3.cloned.1.call-start = ((), (), s32[]{:S(2)}) async-start(), calls=%async_computation.4 | async-start | bytes 3538944 | tf_op jit(solution)/shard_map/reduce_scatter | solution.py:105
  155.3 1.0 copy-start.12
  168.8 1.6 copy-start.3
  168.8 1.9 copy-start.7
  168.8 141.7 %reduce-scatter.5.cloned.1.call-start = ((), (), s32[]{:S(2)}) async-start(), calls=%async_computation.5 | async-start | bytes 9437184 | tf_op jit(solution)/shard_map/reduce_scatter | solution.py:91
  177.0 35.7 %copy-start.2 = (bf16[96,2048]{1,0:T(8,128)(2,1)S(1)}, bf16[96,2048]{1,0:T(8,128)(2,1)}, u32[]{:S(2)}) copy-start(bf16[96,2048]{1,0:T(8,128)(2,1)} %param.14) | copy-start | bytes 1179652
  177.0 35.7 %copy-start.8 = (bf16[1,96,2048]{2,1,0:T(8,128)(2,1)S(1)}, bf16[1,96,2048]{2,1,0:T(8,128)(2,1)}, u32[]{:S(2)}) copy-start(bf16[1,96,2048]{2,1,0:T(8,128)(2,1)} %param.18) | copy-start | bytes 1179652
  177.0 35.7 %copy-start.9 = (bf16[1,96,2048]{2,1,0:T(8,128)(2,1)S(1)}, bf16[1,96,2048]{2,1,0:T(8,128)(2,1)}, u32[]{:S(2)}) copy-start(bf16[1,96,2048]{2,1,0:T(8,128)(2,1)} %param.16) | copy-start | bytes 1179652
  177.0 133.5 %copy-start.1 = (bf16[256,2048]{1,0:T(8,128)(2,1)S(1)}, bf16[256,2048]{1,0:T(8,128)(2,1)}, u32[]{:S(2)}) copy-start(bf16[256,2048]{1,0:T(8,128)(2,1)} %param.15) | copy-start | bytes 3145732
  177.0 133.5 %copy-start.5 = (bf16[1,256,2048]{2,1,0:T(8,128)(2,1)S(1)}, bf16[1,256,2048]{2,1,0:T(8,128)(2,1)}, u32[]{:S(2)}) copy-start(bf16[1,256,2048]{2,1,0:T(8,128)(2,1)} %param.19) | copy-start | bytes 3145732
  177.0 577.5 %all-reduce.3.cloned.1.call-start = ((), (), s32[]{:S(2)}) async-start(), calls=%async_computation.6 | async-start | bytes 5767168 | tf_op jit(solution)/shard_map/psum | solution.py:115
  315.0 439.5 %copy-start.10 = (bf16[96,2048]{1,0:T(8,128)(2,1)S(1)}, bf16[96,2048]{1,0:T(8,128)(2,1)}, u32[]{:S(2)}) copy-start(bf16[96,2048]{1,0:T(8,128)(2,1)} %param.20) | copy-start | bytes 1179652
  315.0 441.9 %copy-start.6 = (bf16[256,2048]{1,0:T(8,128)(2,1)S(1)}, bf16[256,2048]{1,0:T(8,128)(2,1)}, u32[]{:S(2)}) copy-start(bf16[256,2048]{1,0:T(8,128)(2,1)} %param.21) | copy-start | bytes 3145732
  754.5 2.4 copy-start.4
Sparse Core Ops, SparseCore 0:
  9.8 43.3 all-gather.2
  55.0 93.5 all-gather.4
  169.0 43.6 reduce-scatter.2
  215.1 95.3 reduce-scatter.4
  315.2 439.2 all-reduce.2
where the time goes:
time: 767 us; the launch traced here: 765 us
  waiting for transfers between devices  705 us (92%)
  matrix products  28.8 us (4%)
  other arithmetic  14 us (2%)
  between operations  13.9 us (2%)
    psum x1, waiting for transfers between devices, shards(): summed_first, summed_second = lax.psum((delta_first, delta_second), 'wide')  439 us
    reduce_scatter x1, waiting for transfers between devices, shards(): lax.psum_scatter((scale_two * jnp.dot(block.T, embed_half, preferred_elem...  95.3 us
    all_gather x1, waiting for transfers between devices, shards(): second_whole = lax.all_gather(w_second, 'narrow', axis=0, tiled=True)  91 us
    all_gather x1, waiting for transfers between devices, shards(): lax.all_gather(w_first, 'narrow', axis=0, tiled=True)  42.6 us
    reduce_scatter x1, waiting for transfers between devices, shards(): lax.psum_scatter((scale_one * jnp.dot(block.T, hidden_half, preferred_ele...  35.6 us
  transfers between devices with their start and end apart: 5, of which 5 were waited for; matrix products, arithmetic and copies ran while one was open for 2% of the time, Pallas kernels for 0%

commit v1 on v0

--- a/solution.py
+++ b/solution.py
@@ -2,7 +2,9 @@
 
 import jax
 import jax.numpy as jnp
+import numpy as np
 from jax import lax
+from jax.sharding import Mesh
 from jax.sharding import PartitionSpec as P
 
 PIX = 768
@@ -18,6 +20,9 @@
 adam_eps = 1e-08
 rate_outer = 0.7
 momentum_coef = 0.9
+
+WIDE = ("zh", "y", "x")
+NARROW = ("zl", "c")
 
 
 def adam_delta(grads, first_moment, second_moment, weights):
@@ -57,6 +62,23 @@
     return embed_grad.astype(jnp.bfloat16)
 
 
+def wide_mean_update(delta, momentum, weights):
+    sites = lax.axis_size(WIDE)
+    rows, cols = delta.shape
+    piece = cols // sites
+    got = lax.all_to_all(delta, WIDE, 1, 0, tiled=True)
+    mean = jnp.sum(got.reshape(sites, rows, piece), axis=0) / sites
+    start = lax.axis_index(WIDE) * piece
+    mom_piece = lax.dynamic_slice_in_dim(momentum, start, piece, axis=1)
+    w_piece = lax.dynamic_slice_in_dim(weights, start, piece, axis=1)
+    new_piece, vel_piece = outer_update(mean, mom_piece, w_piece)
+    both = jnp.concatenate([new_piece, vel_piece], axis=1)
+    spread = jnp.broadcast_to(both[None], (sites,) + both.shape)
+    back = lax.all_to_all(spread, WIDE, 0, 0, tiled=True)
+    back = back.reshape(sites, rows, 2, piece).transpose(2, 1, 0, 3).reshape(2, rows, cols)
+    return back[0], back[1]
+
+
 def shards(
     tile_pool,
     batch_index,
@@ -77,22 +99,21 @@
     hidden = (
         jnp.dot(
             inputs,
-            lax.all_gather(w_first, "narrow", axis=0, tiled=True),
+            lax.all_gather(w_first, NARROW, axis=0, tiled=True),
             preferred_element_type=jnp.float32,
         )
         * scale_one
     )
     active_full, gelu_back = jax.vjp(jax.nn.gelu, hidden)
     active = active_full.astype(jnp.bfloat16)
-    second_whole = lax.all_gather(w_second, "narrow", axis=0, tiled=True)
+    second_whole = lax.all_gather(w_second, NARROW, axis=0, tiled=True)
     embedded = jnp.dot(active, second_whole, preferred_element_type=jnp.float32) * scale_two
     embed_half = embed_gradient(embedded, partner)
-    block = active
     grad_second = lax.psum_scatter(
-        (scale_two * jnp.dot(block.T, embed_half, preferred_element_type=jnp.float32)).astype(
+        (scale_two * jnp.dot(active.T, embed_half, preferred_element_type=jnp.float32)).astype(
             jnp.bfloat16
         ),
-        "narrow",
+        NARROW,
         scatter_dimension=0,
         tiled=True,
     ).astype(jnp.float32)
@@ -101,40 +122,35 @@
         embed_half, second_whole.T, preferred_element_type=jnp.float32
     )
     hidden_half = gelu_back(active_grad)[0].astype(jnp.bfloat16)
-    block = inputs
     grad_first = lax.psum_scatter(
-        (scale_one * jnp.dot(block.T, hidden_half, preferred_element_type=jnp.float32)).astype(
+        (scale_one * jnp.dot(inputs.T, hidden_half, preferred_element_type=jnp.float32)).astype(
             jnp.bfloat16
         ),
-        "narrow",
+        NARROW,
         scatter_dimension=0,
         tiled=True,
     ).astype(jnp.float32)
     delta_first = adam_delta(grad_first, m_first[0], v_first[0], w_first)
-    sites_count = lax.axis_size("wide")
-    summed_first, summed_second = lax.psum((delta_first, delta_second), "wide")
-    new_first, velocity_first = outer_update(summed_first / sites_count, mom_first, w_first)
-    new_second, velocity_second = outer_update(summed_second / sites_count, mom_second, w_second)
-    return (new_first, new_second, velocity_first, velocity_second)
+    rows_first = delta_first.shape[0]
+    new_w, vel = wide_mean_update(
+        jnp.concatenate([delta_first, delta_second], axis=0),
+        jnp.concatenate([mom_first, mom_second], axis=0),
+        jnp.concatenate([w_first, w_second], axis=0),
+    )
+    return (new_w[:rows_first], new_w[rows_first:], vel[:rows_first], vel[rows_first:])
 
 
 def solution(mesh):
+    zh, y, x = 2, 4, 4
+    devices = np.asarray(mesh.devices)
+    wide, narrow = devices.shape
+    sub = Mesh(devices.reshape(zh, y, x, narrow // 2, 2), WIDE + NARROW)
+    site = P(WIDE, NARROW, None)
+    rows = P(NARROW, None)
     return jax.shard_map(
         shards,
-        mesh=mesh,
-        in_specs=(
-            P("wide", "narrow", None),
-            P("wide", "narrow"),
-            P("wide", "narrow"),
-            P("narrow", None),
-            P("narrow", None),
-            P("wide", "narrow", None),
-            P("wide", "narrow", None),
-            P("wide", "narrow", None),
-            P("wide", "narrow", None),
-            P("narrow", None),
-            P("narrow", None),
-        ),
-        out_specs=(P("narrow", None), P("narrow", None), P("narrow", None), P("narrow", None)),
+        mesh=sub,
+        in_specs=(site, P(WIDE, NARROW), P(WIDE, NARROW), rows, rows, site, site, site, site, rows, rows),
+        out_specs=(rows, rows, rows, rows),
         check_vma=False,
     )

time: 767 us -> 500 us (0.65)
  waiting for transfers between devices: 705 us -> 331 us
  blocking collectives: 0 us -> 78.4 us
  local copies, waits for them, and re-layouts: 3.04 us -> 27 us
  starting transfers between devices: 0.38 us -> 10.5 us
    psum x1 -> x0, waiting for transfers between devices: 439 us -> none  [shards(): summed_first, summed_second = lax.psum((delta_first, delta_second), 'wide')]
    all_to_all x0 -> x1, blocking collectives: none -> 78.4 us  [wide_mean_update(): back = lax.all_to_all(spread, WIDE, 0, 0, tiled=True)]
    all_to_all x0 -> x1, waiting for transfers between devices: none -> 64.7 us  [wide_mean_update(): got = lax.all_to_all(delta, WIDE, 1, 0, tiled=True)]
    unnamed x26 -> x38, local copies, waits for them, and re-layouts: 1.73 us -> 15.9 us
    all_to_all x0 -> x1, starting transfers between devices: none -> 10.2 us  [wide_mean_update(): got = lax.all_to_all(delta, WIDE, 1, 0, tiled=True)]
  transfers between devices with their start and end apart: 5 -> 5, of which waited for: 5 -> 5; matrix products, arithmetic and copies ran while one was open for 2% -> 5% of each run, Pallas kernels for 0% -> 0%
where the time goes in v1:
time: 500 us; the launch traced here: 499 us
  waiting for transfers between devices  331 us (66%)
  blocking collectives  78.4 us (16%)
  matrix products  28.8 us (6%)
  local copies, waits for them, and re-layouts  27 us (5%)
  between operations  13.9 us (3%)
  starting transfers between devices  10.5 us (2%)
  other arithmetic  9.72 us (2%)
    reduce_scatter x1, waiting for transfers between devices, shards(): lax.psum_scatter((scale_two * jnp.dot(active.T, embed_half, preferred_ele...  95.3 us
    all_gather x1, waiting for transfers between devices, shards(): second_whole = lax.all_gather(w_second, NARROW, axis=0, tiled=True)  91 us
    all_to_all x1, blocking collectives, wide_mean_update(): back = lax.all_to_all(spread, WIDE, 0, 0, tiled=True)  78.4 us
    all_to_all x1, waiting for transfers between devices, wide_mean_update(): got = lax.all_to_all(delta, WIDE, 1, 0, tiled=True)  64.7 us
    all_gather x1, waiting for transfers between devices, shards(): lax.all_gather(w_first, NARROW, axis=0, tiled=True)  42.6 us
    reduce_scatter x1, waiting for transfers between devices, shards(): lax.psum_scatter((scale_one * jnp.dot(inputs.T, hidden_half, preferred_el...  35.8 us
    unnamed x38, local copies, waits for them, and re-layouts  15.9 us
    all_to_all x1, starting transfers between devices, wide_mean_update(): got = lax.all_to_all(delta, WIDE, 1, 0, tiled=True)  10.2 us
  transfers between devices with their start and end apart: 5, of which 5 were waited for; matrix products, arithmetic and copies ran while one was open for 5% of the time, Pallas kernels for 0%

profile of v1, /device:TPU:64, one launch (start us, length us, event | category | flops | bytes accessed | tf_op | source)
XLA Modules:
  0.0 499.1 jit_solution(17630639147253046783)
XLA Ops:
  7.2 0.0 all-gather.3.cloned.1.call-start
  7.2 0.7 all-gather.3.cloned.1.call-update
  7.9 0.0 all-gather.5.cloned.1.call-start
  8.0 0.7 all-gather.5.cloned.1.call-update
  8.7 0.0 reduce-scatter.3.cloned.1.call-start
  8.7 0.7 compare_select_fusion
  9.4 1.2 gather_fusion
  10.6 42.6 %all-gather.3.cloned.1.call-done = bf16[768,2048]{1,0:T(8,128)(2,1)} async-done(((bf16[96,2048]{1,0:T(8,128)(2,1)}), bf16[768,2048]{1,0:T(8,128)(2,1)}) %all-gather.3.cloned.1.call-update) | async-done | bytes 3145744 | tf_op jit(solution)/shard_map/all_gather | solution.py:102
  53.2 4.4 convolution_multiply_fusion.1
  57.6 91.0 %all-gather.5.cloned.1.call-done = bf16[2048,2048]{1,0:T(8,128)(2,1)} async-done(((bf16[256,2048]{1,0:T(8,128)(2,1)}), bf16[2048,2048]{1,0:T(8,128)(2,1)}) %all-gather.5.cloned.1.call-update) | async-done | bytes 8388624 | tf_op jit(solution)/shard_map/all_gather | solution.py:109
  148.6 6.7 %multiply_reduce_fusion.1 = (f32[256]{0:T(256)S(1)}, f32[256,2048]{1,0:T(8,128)S(1)}) fusion(bf16[2048,2048]{1,0:T(8,128)(2,1)} %all-gather.5.cloned.1.call-done, f32[256,2048]{1,0:T(8,128)} %convolution_multiply_fusion.1), kind=kOutput, calls=%fused_computation.27 | convolution fusion | flops 2153774848 | bytes 12583936 | tf_op jit(solution)/shard_map/dot_general | solution.py:110
  155.3 0.6 convolution_multiply_fusion.3
  155.9 0.1 copy.25
  156.0 0.1 fusion.35
  156.1 0.2 fusion.36
  156.3 0.8 multiply_reduce_fusion
  157.1 1.5 multiply_convert_fusion.2
  158.6 10.2 %multiply_convert_fusion.1 = bf16[768,2048]{1,0:T(8,128)(2,1)} fusion(f32[256,2048]{1,0:T(8,128)} %convolution_multiply_fusion.1, bf16[256,2048]{1,0:T(8,128)(2,1)} %multiply_convert_fusion.2, bf16[2048,2048]{1,0:T(8,128)(2,1)} %all-gather.5.cloned.1.call-done, bf16[256,768]{1,0:T(8,128)(2,1)S(1)} %gather_fusion, pred[256]{0:T(512)(128)(4,1)S(1)} %compare_and_fusion), kind=kOutput, calls=%fused_computation.2 | convolution fusion | flops 2967142400 | bytes 15073536 | tf_op jit(solution)/shard_map/dot_general | solution.py:126
  168.8 0.0 reduce-scatter.3.cloned.1.call-update
  168.8 0.2 reduce-scatter.5.cloned.1.call-start
  169.1 1.3 copy-done.6
  170.4 0.3 copy-done.10
  170.7 6.2 %multiply_convert_fusion = bf16[2048,2048]{1,0:T(8,128)(2,1)} fusion(bf16[256,2048]{1,0:T(8,128)(2,1)S(1)} %copy-done.10, f32[256,2048]{1,0:T(8,128)S(1)} %copy-done.6), kind=kOutput, calls=%fused_computation.1 | convolution fusion | flops 2160590848 | bytes 11534336 | tf_op jit(solution)/shard_map/dot_general | solution.py:113
  176.9 0.0 reduce-scatter.5.cloned.1.call-update
  176.9 35.8 %reduce-scatter.3.cloned.1.call-done = bf16[96,2048]{1,0:T(8,128)(2,1)} async-done(((bf16[768,2048]{1,0:T(8,128)(2,1)}), bf16[96,2048]{1,0:T(8,128)(2,1)}) %reduce-scatter.3.cloned.1.call-update) | async-done | bytes 393232 | tf_op jit(solution)/shard_map/reduce_scatter | solution.py:125
  212.7 2.5 fusion.24
  215.2 95.3 %reduce-scatter.5.cloned.1.call-done = bf16[256,2048]{1,0:T(8,128)(2,1)} async-done(((bf16[2048,2048]{1,0:T(8,128)(2,1)}), bf16[256,2048]{1,0:T(8,128)(2,1)}) %reduce-scatter.5.cloned.1.call-update) | async-done | bytes 1048592 | tf_op jit(solution)/shard_map/reduce_scatter | solution.py:112
  310.5 3.2 fusion.3
  313.7 0.3 pad_maximum_fusion
  314.1 2.3 copy.26
  316.4 10.2 %all-to-all-start = ((f32[352,32,64]{0,2,1:T(8,128)}), f32[352,32,64]{0,2,1:T(8,128)S(1)}, u32[]{:S(2)}, u32[]{:S(2)}) async-start(f32[352,32,64]{0,2,1:T(8,128)} %bitcast.45), calls=%async_computation.2 | async-start | bytes 6291456 | tf_op jit(solution)/shard_map/all_to_all | solution.py:69
  326.6 2.0 copy.23
  328.6 2.3 copy.24
  330.9 2.0 copy.27
  332.9 2.3 copy.28
  335.1 64.7 %all-to-all-done = f32[352,32,64]{0,2,1:T(8,128)S(1)} async-done(((f32[352,32,64]{0,2,1:T(8,128)}), f32[352,32,64]{0,2,1:T(8,128)S(1)}, u32[]{:S(2)}, u32[]{:S(2)}) %all-to-all-start) | async-done | bytes 2883616 | tf_op jit(solution)/shard_map/all_to_all | solution.py:69
  399.8 0.2 reduce_sum.39
  399.9 0.9 subtract_convert_fusion
  400.9 0.1 copy.29
  401.0 0.4 broadcast_in_dim.30
  401.4 78.4 %all_to_all.18 = bf16[32,352,128]{2,1,0:T(8,128)(2,1)} all-to-all(bf16[32,352,128]{2,1,0:T(8,128)(2,1)S(1)} %broadcast_in_dim.30), channel_id=1, replica_groups=mesh['zh'=2,'y'=4,'x'=4,'zl'=4,'c'=2] {'zh','y','x'}, dimensions={0} | all-to-all | bytes 5767168 | tf_op jit(solution)/shard_map/all_to_all | solution.py:77
  479.9 3.4 copy.30
  483.2 1.2 fusion.61
  484.4 2.4 fusion.60
  486.8 2.4 copy.34
  489.2 1.4 copy.32
  490.7 1.0 copy.33
  491.6 1.0 copy.31
  (33 shorter events, 0.1 us)
Async XLA Ops:
  7.2 2.3 copy-start
  7.2 46.0 %all-gather.3.cloned.1.call-start = ((), (), s32[]{:S(2)}) async-start(), calls=%async_computation.4 | async-start | bytes 3538944 | tf_op jit(solution)/shard_map/all_gather | solution.py:102
  7.9 2.7 copy-start.13
  7.9 140.7 %all-gather.5.cloned.1.call-start = ((), (), s32[]{:S(2)}) async-start(), calls=%async_computation.5 | async-start | bytes 9437184 | tf_op jit(solution)/shard_map/all_gather | solution.py:109
  8.7 204.0 %reduce-scatter.3.cloned.1.call-start = ((), (), s32[]{:S(2)}) async-start(), calls=%async_computation.6 | async-start | bytes 3538944 | tf_op jit(solution)/shard_map/reduce_scatter | solution.py:125
  155.3 1.0 copy-start.14
  168.8 1.6 copy-start.6
  168.8 1.9 copy-start.10
  168.8 141.6 %reduce-scatter.5.cloned.1.call-start = ((), (), s32[]{:S(2)}) async-start(), calls=%async_computation.7 | async-start | bytes 9437184 | tf_op jit(solution)/shard_map/reduce_scatter | solution.py:112
  176.9 35.8 %copy-start.4 = (bf16[96,2048]{1,0:T(8,128)(2,1)S(1)}, bf16[96,2048]{1,0:T(8,128)(2,1)}, u32[]{:S(2)}) copy-start(bf16[96,2048]{1,0:T(8,128)(2,1)} %param.14) | copy-start | bytes 1179652
  176.9 35.8 %copy-start.11 = (bf16[1,96,2048]{2,1,0:T(8,128)(2,1)S(1)}, bf16[1,96,2048]{2,1,0:T(8,128)(2,1)}, u32[]{:S(2)}) copy-start(bf16[1,96,2048]{2,1,0:T(8,128)(2,1)} %param.18) | copy-start | bytes 1179652
  176.9 35.8 %copy-start.12 = (bf16[1,96,2048]{2,1,0:T(8,128)(2,1)S(1)}, bf16[1,96,2048]{2,1,0:T(8,128)(2,1)}, u32[]{:S(2)}) copy-start(bf16[1,96,2048]{2,1,0:T(8,128)(2,1)} %param.16) | copy-start | bytes 1179652
  176.9 133.6 %copy-start.2 = (bf16[256,2048]{1,0:T(8,128)(2,1)S(1)}, bf16[256,2048]{1,0:T(8,128)(2,1)}, u32[]{:S(2)}) copy-start(bf16[256,2048]{1,0:T(8,128)(2,1)} %param.15) | copy-start | bytes 3145732
  176.9 133.6 %copy-start.9 = (bf16[1,256,2048]{2,1,0:T(8,128)(2,1)S(1)}, bf16[1,256,2048]{2,1,0:T(8,128)(2,1)}, u32[]{:S(2)}) copy-start(bf16[1,256,2048]{2,1,0:T(8,128)(2,1)} %param.19) | copy-start | bytes 3145732
  310.5 3.2 copy-start.5
  316.4 83.4 %all-to-all-start = ((f32[352,32,64]{0,2,1:T(8,128)}), f32[352,32,64]{0,2,1:T(8,128)S(1)}, u32[]{:S(2)}, u32[]{:S(2)}) async-start(f32[352,32,64]{0,2,1:T(8,128)} %bitcast.45), calls=%async_computation.2 | async-start | bytes 6291456 | tf_op jit(solution)/shard_map/all_to_all | solution.py:69
  486.8 2.4 copy-start.3
  486.8 3.8 copy-start.8
  486.8 4.8 copy-start.7
  486.8 5.8 %copy-start.1 = (bf16[1,128,768]{2,1,0:T(8,128)(2,1)S(1)}, bf16[1,128,768]{2,1,0:T(8,128)(2,1)}, u32[]{:S(2)}) copy-start(bf16[1,128,768]{2,1,0:T(8,128)(2,1)} %param.11) | copy-start | bytes 589828
Sparse Core Ops, SparseCore 0:
  9.8 43.3 all-gather.2
  55.0 93.5 all-gather.4
  169.0 43.6 reduce-scatter.2
  215.1 95.3 reduce-scatter.4

commit v2 on v1

--- a/solution.py
+++ b/solution.py
@@ -62,20 +62,22 @@
     return embed_grad.astype(jnp.bfloat16)
 
 
-def wide_mean_update(delta, momentum, weights):
+def wide_mean_update(delta, momentum, weights, axis):
     sites = lax.axis_size(WIDE)
-    rows, cols = delta.shape
-    piece = cols // sites
-    got = lax.all_to_all(delta, WIDE, 1, 0, tiled=True)
-    mean = jnp.sum(got.reshape(sites, rows, piece), axis=0) / sites
+    piece = delta.shape[axis] // sites
+    got = lax.all_to_all(delta, WIDE, axis, axis, tiled=True)
+    got = jnp.moveaxis(got, axis, 0).reshape((sites, piece) + (delta.shape[1 - axis],))
+    mean = jnp.moveaxis(jnp.sum(got, axis=0), 0, axis) / sites
     start = lax.axis_index(WIDE) * piece
-    mom_piece = lax.dynamic_slice_in_dim(momentum, start, piece, axis=1)
-    w_piece = lax.dynamic_slice_in_dim(weights, start, piece, axis=1)
+    mom_piece = lax.dynamic_slice_in_dim(momentum, start, piece, axis=axis)
+    w_piece = lax.dynamic_slice_in_dim(weights, start, piece, axis=axis)
     new_piece, vel_piece = outer_update(mean, mom_piece, w_piece)
-    both = jnp.concatenate([new_piece, vel_piece], axis=1)
+    both = jnp.stack([new_piece, vel_piece], axis=0)
     spread = jnp.broadcast_to(both[None], (sites,) + both.shape)
     back = lax.all_to_all(spread, WIDE, 0, 0, tiled=True)
-    back = back.reshape(sites, rows, 2, piece).transpose(2, 1, 0, 3).reshape(2, rows, cols)
+    back = jnp.moveaxis(back, 0, 1 + axis)
+    shape = list(delta.shape)
+    back = back.reshape([2] + shape)
     return back[0], back[1]
 
 
@@ -109,15 +111,6 @@
     second_whole = lax.all_gather(w_second, NARROW, axis=0, tiled=True)
     embedded = jnp.dot(active, second_whole, preferred_element_type=jnp.float32) * scale_two
     embed_half = embed_gradient(embedded, partner)
-    grad_second = lax.psum_scatter(
-        (scale_two * jnp.dot(active.T, embed_half, preferred_element_type=jnp.float32)).astype(
-            jnp.bfloat16
-        ),
-        NARROW,
-        scatter_dimension=0,
-        tiled=True,
-    ).astype(jnp.float32)
-    delta_second = adam_delta(grad_second, m_second[0], v_second[0], w_second)
     active_grad = scale_two * jnp.dot(
         embed_half, second_whole.T, preferred_element_type=jnp.float32
     )
@@ -131,13 +124,26 @@
         tiled=True,
     ).astype(jnp.float32)
     delta_first = adam_delta(grad_first, m_first[0], v_first[0], w_first)
-    rows_first = delta_first.shape[0]
-    new_w, vel = wide_mean_update(
-        jnp.concatenate([delta_first, delta_second], axis=0),
-        jnp.concatenate([mom_first, mom_second], axis=0),
-        jnp.concatenate([w_first, w_second], axis=0),
-    )
-    return (new_w[:rows_first], new_w[rows_first:], vel[:rows_first], vel[rows_first:])
+    new_first, vel_first = wide_mean_update(delta_first, mom_first, w_first, 1)
+    term_second = (
+        scale_two * jnp.dot(active.T, embed_half, preferred_element_type=jnp.float32)
+    ).astype(jnp.bfloat16)
+    halves = []
+    cols = term_second.shape[1] // 2
+    for h in range(2):
+        part = slice(h * cols, (h + 1) * cols)
+        grad_part = lax.psum_scatter(
+            term_second[:, part], NARROW, scatter_dimension=0, tiled=True
+        ).astype(jnp.float32)
+        delta_part = adam_delta(
+            grad_part, m_second[0][:, part], v_second[0][:, part], w_second[:, part]
+        )
+        halves.append(
+            wide_mean_update(delta_part, mom_second[:, part], w_second[:, part], 0)
+        )
+    new_second = jnp.concatenate([halves[0][0], halves[1][0]], axis=1)
+    vel_second = jnp.concatenate([halves[0][1], halves[1][1]], axis=1)
+    return (new_first, new_second, vel_first, vel_second)
 
 
 def solution(mesh):

time: 500 us -> 525 us (1.050)
  waiting for transfers between devices: 331 us -> 375 us
  blocking collectives: 78.4 us -> 42.4 us
  starting transfers between devices: 10.5 us -> 29.1 us
  other arithmetic: 9.72 us -> 15 us
    all_to_all x1, blocking collectives: 78.4 us -> 42.4 us  [wide_mean_update(): got = lax.all_to_all(delta, WIDE, axis, axis, tiled=True)]
    reduce_scatter x1 -> x2, waiting for transfers between devices: 95.3 us -> 121 us  [shards(): lax.psum_scatter(term_second[:, part], NARROW, scatter_dimension=0, tiled...]
    all_to_all x1 -> x5, waiting for transfers between devices: 64.7 us -> 84.3 us  [the longest x3 64.1 us: wide_mean_update(): back = lax.all_to_all(spread, WIDE, 0, 0, tiled=True)]
    all_to_all x1 -> x5, starting transfers between devices: 10.2 us -> 28.7 us  [the longest x2 14.6 us: wide_mean_update(): got = lax.all_to_all(delta, WIDE, axis, axis, tiled=True)]
    unnamed x38 -> x28, local copies, waits for them, and re-layouts: 15.9 us -> 7.29 us
  transfers between devices with their start and end apart: 5 -> 10, of which waited for: 5 -> 9; matrix products, arithmetic and copies ran while one was open for 5% -> 6% of each run, Pallas kernels for 0% -> 0%
where the time goes in v2:
time: 525 us; the launch traced here: 524 us
  waiting for transfers between devices  375 us (71%)
  blocking collectives  42.4 us (8%)
  starting transfers between devices  29.1 us (6%)
  matrix products  25.5 us (5%)
  local copies, waits for them, and re-layouts  22.6 us (4%)
  other arithmetic  15 us (3%)
  between operations  14 us (3%)
    reduce_scatter x2, waiting for transfers between devices, shards(): lax.psum_scatter(term_second[:, part], NARROW, scatter_dimension=0, tiled...  121 us
    all_gather x1, waiting for transfers between devices, shards(): second_whole = lax.all_gather(w_second, NARROW, axis=0, tiled=True)  91 us
    all_to_all x3, waiting for transfers between devices, wide_mean_update(): back = lax.all_to_all(spread, WIDE, 0, 0, tiled=True)  64.1 us
    all_gather x1, waiting for transfers between devices, shards(): lax.all_gather(w_first, NARROW, axis=0, tiled=True)  42.6 us
    all_to_all x1, blocking collectives, wide_mean_update(): got = lax.all_to_all(delta, WIDE, axis, axis, tiled=True)  42.4 us
    reduce_scatter x1, waiting for transfers between devices, shards(): lax.psum_scatter((scale_one * jnp.dot(inputs.T, hidden_half, preferred_el...  34.6 us
    all_to_all x2, waiting for transfers between devices, wide_mean_update(): got = lax.all_to_all(delta, WIDE, axis, axis, tiled=True)  20.2 us
    all_to_all x2, starting transfers between devices, wide_mean_update(): got = lax.all_to_all(delta, WIDE, axis, axis, tiled=True)  14.6 us
  transfers between devices with their start and end apart: 10, of which 9 were waited for; matrix products, arithmetic and copies ran while one was open for 6% of the time, Pallas kernels for 0%

profile of v2, /device:TPU:64, one launch (start us, length us, event | category | flops | bytes accessed | tf_op | source)
XLA Modules:
  0.0 523.8 jit_solution(6939493928089359772)
XLA Ops:
  7.2 0.7 all-gather.3.cloned.1.call-update
  8.0 0.7 all-gather.5.cloned.1.call-update
  8.7 0.7 compare_select_fusion
  9.4 1.2 gather_fusion
  10.6 42.6 %all-gather.3.cloned.1.call-done = bf16[768,2048]{1,0:T(8,128)(2,1)} async-done(((bf16[96,2048]{1,0:T(8,128)(2,1)}), bf16[768,2048]{1,0:T(8,128)(2,1)}) %all-gather.3.cloned.1.call-update) | async-done | bytes 3145744 | tf_op jit(solution)/shard_map/all_gather | solution.py:104
  53.2 4.4 convolution_multiply_fusion.1
  57.6 91.0 %all-gather.5.cloned.1.call-done = bf16[2048,2048]{1,0:T(8,128)(2,1)} async-done(((bf16[256,2048]{1,0:T(8,128)(2,1)}), bf16[2048,2048]{1,0:T(8,128)(2,1)}) %all-gather.5.cloned.1.call-update) | async-done | bytes 8388624 | tf_op jit(solution)/shard_map/all_gather | solution.py:111
  148.6 6.7 %multiply_reduce_fusion.1 = (f32[256]{0:T(256)S(1)}, f32[256,2048]{1,0:T(8,128)S(1)}) fusion(bf16[2048,2048]{1,0:T(8,128)(2,1)} %all-gather.5.cloned.1.call-done, f32[256,2048]{1,0:T(8,128)} %convolution_multiply_fusion.1), kind=kOutput, calls=%fused_computation.17 | convolution fusion | flops 2153774848 | bytes 12583936 | tf_op jit(solution)/shard_map/dot_general | solution.py:112
  156.4 0.8 multiply_reduce_fusion
  157.1 1.5 multiply_convert_fusion.2
  158.6 10.1 %multiply_convert_fusion.1 = bf16[768,2048]{1,0:T(8,128)(2,1)} fusion(f32[256,2048]{1,0:T(8,128)} %convolution_multiply_fusion.1, bf16[256,2048]{1,0:T(8,128)(2,1)} %multiply_convert_fusion.2, bf16[2048,2048]{1,0:T(8,128)(2,1)} %all-gather.5.cloned.1.call-done, bf16[256,768]{1,0:T(8,128)(2,1)S(1)} %gather_fusion, pred[256]{0:T(512)(128)(4,1)S(1)} %compare_and_fusion), kind=kOutput, calls=%fused_computation.2 | convolution fusion | flops 2967142400 | bytes 15073536 | tf_op jit(solution)/shard_map/dot_general | solution.py:119
  169.1 1.3 copy-done.4
  170.7 3.0 multiply_convert_fusion
  173.6 3.8 fusion.77
  178.0 34.6 %reduce-scatter.4.cloned.1.call-done = bf16[96,2048]{1,0:T(8,128)(2,1)} async-done(((bf16[768,2048]{1,0:T(8,128)(2,1)}), bf16[96,2048]{1,0:T(8,128)(2,1)}) %reduce-scatter.4.cloned.1.call-update) | async-done | bytes 393232 | tf_op jit(solution)/shard_map/reduce_scatter | solution.py:118
  212.7 1.6 fusion.33
  214.3 1.3 copy.23
  215.6 9.9 %all-to-all-start = ((f32[96,32,64]{0,2,1:T(8,128)}), f32[96,32,64]{0,2,1:T(8,128)S(1)}, u32[]{:S(2)}, u32[]{:S(2)}) async-start(f32[96,32,64]{0,2,1:T(8,128)} %bitcast.8), calls=%async_computation.1 | async-start | bytes 2097152 | tf_op jit(solution)/shard_map/all_to_all | solution.py:68
  225.6 66.0 %reduce-scatter.6.cloned.1.call-done = bf16[256,1024]{1,0:T(8,128)(2,1)} async-done(((bf16[2048,1024]{1,0:T(8,128)(2,1)}), bf16[256,1024]{1,0:T(8,128)(2,1)}) %reduce-scatter.6.cloned.1.call-update) | async-done | bytes 524304 | tf_op jit(solution)/shard_map/reduce_scatter | solution.py:135
  291.5 54.9 %reduce-scatter.8.cloned.1.call-done = bf16[256,1024]{1,0:T(8,128)(2,1)} async-done(((bf16[2048,1024]{1,0:T(8,128)(2,1)}), bf16[256,1024]{1,0:T(8,128)(2,1)}) %reduce-scatter.8.cloned.1.call-update) | async-done | bytes 524304 | tf_op jit(solution)/shard_map/reduce_scatter | solution.py:135
  346.5 4.4 fusion.11
  350.9 1.0 copy-done.3
  351.9 42.4 %all_to_all.45 = f32[32,8,1024]{2,1,0:T(8,128)S(1)} all-to-all(f32[32,8,1024]{2,1,0:T(8,128)S(1)} %get-tuple-element.14), channel_id=1, replica_groups=mesh['zh'=2,'y'=4,'x'=4,'zl'=4,'c'=2] {'zh','y','x'}, dimensions={0} | all-to-all | bytes 2097152 | tf_op jit(solution)/shard_map/all_to_all | solution.py:68
  394.3 4.7 all-to-all-start.4
  399.0 0.7 constant_dynamic-slice_fusion
  399.7 0.8 copy.28
  400.5 1.4 constant_dynamic-slice_fusion.1
  401.9 1.4 copy.27
  403.4 1.3 bitcast_reduce_fusion
  404.7 0.7 fusion.65
  406.0 20.2 %all-to-all-done.4 = f32[32,8,1024]{2,1,0:T(8,128)S(1)} async-done(((f32[32,8,1024]{2,1,0:T(8,128)}), f32[32,8,1024]{2,1,0:T(8,128)S(1)}, u32[]{:S(2)}, u32[]{:S(2)}) %all-to-all-start.4) | async-done | bytes 1048608 | tf_op jit(solution)/shard_map/all_to_all | solution.py:68
  426.2 2.0 broadcast_in_dim.23
  428.2 4.7 all-to-all-start.1
  432.9 1.1 fusion.79
  434.6 0.7 reduce_sum.58
  435.4 0.8 fusion.62
  436.2 21.0 %all-to-all-done.1 = bf16[32,2,96,64]{2,3,1,0:T(8,128)(2,1)} async-done(((bf16[32,2,96,64]{2,3,1,0:T(8,128)(2,1)}), bf16[32,2,96,64]{2,3,1,0:T(8,128)(2,1)}, u32[]{:S(2)}, u32[]{:S(2)}) %all-to-all-start.1) | async-done | bytes 786464 | tf_op jit(solution)/shard_map/all_to_all | solution.py:77
  457.1 1.1 broadcast_in_dim.25
  458.2 4.4 all-to-all-start.5
  462.7 22.9 %all-to-all-done.5 = bf16[32,2,8,1024]{3,2,1,0:T(8,128)(2,1)S(1)} async-done(((bf16[32,2,8,1024]{3,2,1,0:T(8,128)(2,1)}), bf16[32,2,8,1024]{3,2,1,0:T(8,128)(2,1)S(1)}, u32[]{:S(2)}, u32[]{:S(2)}) %all-to-all-start.5) | async-done | bytes 1048608 | tf_op jit(solution)/shard_map/all_to_all | solution.py:77
  485.6 1.1 broadcast_in_dim.24
  486.7 4.9 all-to-all-start.3
  491.6 1.3 fusion.78
  492.9 1.0 copy.25
  493.9 1.0 copy.26
  494.9 20.2 %all-to-all-done.3 = bf16[32,2,8,1024]{3,2,1,0:T(8,128)(2,1)S(1)} async-done(((bf16[32,2,8,1024]{3,2,1,0:T(8,128)(2,1)}), bf16[32,2,8,1024]{3,2,1,0:T(8,128)(2,1)S(1)}, u32[]{:S(2)}, u32[]{:S(2)}) %all-to-all-start.3) | async-done | bytes 1048608 | tf_op jit(solution)/shard_map/all_to_all | solution.py:77
  515.2 1.1 pad_maximum_fusion
  516.3 1.1 pad_maximum_fusion.1
  (45 shorter events, 3.7 us)
Async XLA Ops:
  7.2 391.8 %copy-start = (bf16[96,2048]{1,0:T(8,128)(2,1)S(1)}, bf16[96,2048]{1,0:T(8,128)(2,1)}, u32[]{:S(2)}) copy-start(bf16[96,2048]{1,0:T(8,128)(2,1)} %param.20) | copy-start | bytes 1179652
  7.2 2.2 copy-start.1
  7.2 46.0 %all-gather.3.cloned.1.call-start = ((), (), s32[]{:S(2)}) async-start(), calls=%async_computation.9 | async-start | bytes 3538944 | tf_op jit(solution)/shard_map/all_gather | solution.py:104
  7.9 2.7 copy-start.10
  7.9 140.7 %all-gather.5.cloned.1.call-start = ((), (), s32[]{:S(2)}) async-start(), calls=%async_computation.10 | async-start | bytes 9437184 | tf_op jit(solution)/shard_map/all_gather | solution.py:111
  8.7 204.0 %reduce-scatter.4.cloned.1.call-start = ((), (), s32[]{:S(2)}) async-start(), calls=%async_computation.11 | async-start | bytes 3538944 | tf_op jit(solution)/shard_map/reduce_scatter | solution.py:118
  155.3 1.0 copy-start.11
  168.8 1.6 copy-start.4
  168.8 1.9 copy-start.7
  168.8 122.7 %reduce-scatter.6.cloned.1.call-start = ((), (), s32[]{:S(2)}) async-start(), calls=%async_computation.12 | async-start | bytes 4718592 | tf_op jit(solution)/shard_map/reduce_scatter | solution.py:135
  177.4 169.0 %reduce-scatter.8.cloned.1.call-start = ((), (), s32[]{:S(2)}) async-start(), calls=%async_computation.13 | async-start | bytes 4718592 | tf_op jit(solution)/shard_map/reduce_scatter | solution.py:135
  177.5 35.2 %copy-start.5 = (bf16[96,2048]{1,0:T(8,128)(2,1)S(1)}, bf16[96,2048]{1,0:T(8,128)(2,1)}, u32[]{:S(2)}) copy-start(bf16[96,2048]{1,0:T(8,128)(2,1)} %param.14) | copy-start | bytes 1179652
  177.5 35.2 %copy-start.8 = (bf16[1,96,2048]{2,1,0:T(8,128)(2,1)S(1)}, bf16[1,96,2048]{2,1,0:T(8,128)(2,1)}, u32[]{:S(2)}) copy-start(bf16[1,96,2048]{2,1,0:T(8,128)(2,1)} %param.18) | copy-start | bytes 1179652
  177.5 35.2 %copy-start.9 = (bf16[1,96,2048]{2,1,0:T(8,128)(2,1)S(1)}, bf16[1,96,2048]{2,1,0:T(8,128)(2,1)}, u32[]{:S(2)}) copy-start(bf16[1,96,2048]{2,1,0:T(8,128)(2,1)} %param.16) | copy-start | bytes 1179652
  214.3 132.1 %copy-start.2 = (bf16[256,2048]{1,0:T(8,128)(2,1)S(1)}, bf16[256,2048]{1,0:T(8,128)(2,1)}, u32[]{:S(2)}) copy-start(bf16[256,2048]{1,0:T(8,128)(2,1)} %param.15) | copy-start | bytes 3145732
  215.6 135.3 %all-to-all-start = ((f32[96,32,64]{0,2,1:T(8,128)}), f32[96,32,64]{0,2,1:T(8,128)S(1)}, u32[]{:S(2)}, u32[]{:S(2)}) async-start(f32[96,32,64]{0,2,1:T(8,128)} %bitcast.8), calls=%async_computation.1 | async-start | bytes 2097152 | tf_op jit(solution)/shard_map/all_to_all | solution.py:68
  350.9 1.0 copy-start.3
  394.3 32.0 %all-to-all-start.4 = ((f32[32,8,1024]{2,1,0:T(8,128)}), f32[32,8,1024]{2,1,0:T(8,128)S(1)}, u32[]{:S(2)}, u32[]{:S(2)}) async-start(f32[32,8,1024]{2,1,0:T(8,128)} %get-tuple-element.15), calls=%async_computation.7 | async-start | bytes 2097152 | tf_op jit(solution)/shard_map/all_to_all | solution.py:68
  428.2 28.9 %all-to-all-start.1 = ((bf16[32,2,96,64]{2,3,1,0:T(8,128)(2,1)}), bf16[32,2,96,64]{2,3,1,0:T(8,128)(2,1)}, u32[]{:S(2)}, u32[]{:S(2)}) async-start(bf16[32,2,96,64]{2,3,1,0:T(8,128)(2,1)} %broadcast_in_dim.23), calls=%async_computation.2 | async-start | bytes 2097152 | tf_op jit(solution)/shard_map/all_to_all | solution.py:77
  432.9 1.6 copy-start.6
  458.2 27.4 %all-to-all-start.5 = ((bf16[32,2,8,1024]{3,2,1,0:T(8,128)(2,1)}), bf16[32,2,8,1024]{3,2,1,0:T(8,128)(2,1)S(1)}, u32[]{:S(2)}, u32[]{:S(2)}) async-start(bf16[32,2,8,1024]{3,2,1,0:T(8,128)(2,1)} %broadcast_in_dim.25), calls=%async_computation.8 | async-start | bytes 2097152 | tf_op jit(solution)/shard_map/all_to_all | solution.py:77
  486.7 28.4 %all-to-all-start.3 = ((bf16[32,2,8,1024]{3,2,1,0:T(8,128)(2,1)}), bf16[32,2,8,1024]{3,2,1,0:T(8,128)(2,1)S(1)}, u32[]{:S(2)}, u32[]{:S(2)}) async-start(bf16[32,2,8,1024]{3,2,1,0:T(8,128)(2,1)} %broadcast_in_dim.24), calls=%async_computation.5 | async-start | bytes 2097152 | tf_op jit(solution)/shard_map/all_to_all | solution.py:77
Sparse Core Ops, SparseCore 0:
  9.8 43.3 all-gather.2
  55.0 93.5 all-gather.4
  168.9 43.6 reduce-scatter.3
  215.1 76.4 reduce-scatter.5
  293.9 52.4 reduce-scatter.7

commit v3 on v1

--- a/solution.py
+++ b/solution.py
@@ -79,6 +79,26 @@
     return back[0], back[1]
 
 
+def gather_weights(w_first, w_second):
+    halves = lax.axis_size("zh")
+    h = lax.axis_index("zh")
+    shards_n = lax.axis_size(NARROW)
+    r1 = w_first.shape[0] // halves
+    r2 = w_second.shape[0] // halves
+    mine = jnp.concatenate(
+        [
+            lax.dynamic_slice_in_dim(w_first, h * r1, r1, axis=0),
+            lax.dynamic_slice_in_dim(w_second, h * r2, r2, axis=0),
+        ],
+        axis=0,
+    )
+    got = lax.all_gather(mine, ("zh",) + NARROW, axis=0, tiled=False)
+    got = got.reshape(halves, shards_n, r1 + r2, got.shape[-1]).transpose(1, 0, 2, 3)
+    first = got[:, :, :r1].reshape(shards_n * halves * r1, -1)
+    second = got[:, :, r1:].reshape(shards_n * halves * r2, -1)
+    return first, second
+
+
 def shards(
     tile_pool,
     batch_index,
@@ -96,17 +116,10 @@
     partner = pair_label[0]
     scale_one = 1.0 / math.sqrt(PIX)
     scale_two = 1.0 / math.sqrt(MID)
-    hidden = (
-        jnp.dot(
-            inputs,
-            lax.all_gather(w_first, NARROW, axis=0, tiled=True),
-            preferred_element_type=jnp.float32,
-        )
-        * scale_one
-    )
+    first_whole, second_whole = gather_weights(w_first, w_second)
+    hidden = jnp.dot(inputs, first_whole, preferred_element_type=jnp.float32) * scale_one
     active_full, gelu_back = jax.vjp(jax.nn.gelu, hidden)
     active = active_full.astype(jnp.bfloat16)
-    second_whole = lax.all_gather(w_second, NARROW, axis=0, tiled=True)
     embedded = jnp.dot(active, second_whole, preferred_element_type=jnp.float32) * scale_two
     embed_half = embed_gradient(embedded, partner)
     grad_second = lax.psum_scatter(

time: 500 us -> 456 us (0.912)
  waiting for transfers between devices: 331 us -> 262 us
  local copies, waits for them, and re-layouts: 27 us -> 48.9 us
    all_gather x2 -> x1, waiting for transfers between devices: 134 us -> 69.2 us  [gather_weights(): got = lax.all_gather(mine, ('zh',) + NARROW, axis=0, tiled=False)]
    slice x0 -> x4, local copies, waits for them, and re-layouts: none -> 19.2 us  [the longest x2 16.6 us: gather_weights(): second = got[:, :, r1:].reshape(shards_n * halves * r2, -1)]
    unnamed x38 -> x42, local copies, waits for them, and re-layouts: 15.9 us -> 15.9 us
  transfers between devices with their start and end apart: 5 -> 4, of which waited for: 5 -> 4; matrix products, arithmetic and copies ran while one was open for 5% -> 4% of each run, Pallas kernels for 0% -> 0%
where the time goes in v3:
time: 456 us; the launch traced here: 451 us
  waiting for transfers between devices  262 us (57%)
  blocking collectives  80.2 us (18%)
  local copies, waits for them, and re-layouts  48.9 us (11%)
  matrix products  25.6 us (6%)
  between operations  14 us (3%)
  starting transfers between devices  10.5 us (2%)
  other arithmetic  9.94 us (2%)
    reduce_scatter x1, waiting for transfers between devices, shards(): lax.psum_scatter((scale_two * jnp.dot(active.T, embed_half, preferred_ele...  95.4 us
    all_to_all x1, blocking collectives, wide_mean_update(): back = lax.all_to_all(spread, WIDE, 0, 0, tiled=True)  80.2 us
    all_gather x1, waiting for transfers between devices, gather_weights(): got = lax.all_gather(mine, ('zh',) + NARROW, axis=0, tiled=False)  69.2 us
    all_to_all x1, waiting for transfers between devices, wide_mean_update(): got = lax.all_to_all(delta, WIDE, 1, 0, tiled=True)  62.7 us
    reduce_scatter x1, waiting for transfers between devices, shards(): lax.psum_scatter((scale_one * jnp.dot(inputs.T, hidden_half, preferred_el...  34.8 us
    slice x2, local copies, waits for them, and re-layouts, gather_weights(): second = got[:, :, r1:].reshape(shards_n * halves * r2, -1)  16.6 us
    unnamed x42, local copies, waits for them, and re-layouts  15.9 us
    all_to_all x1, starting transfers between devices, wide_mean_update(): got = lax.all_to_all(delta, WIDE, 1, 0, tiled=True)  10.2 us
  transfers between devices with their start and end apart: 4, of which 4 were waited for; matrix products, arithmetic and copies ran while one was open for 4% of the time, Pallas kernels for 0%

profile of v3, /device:TPU:64, one launch (start us, length us, event | category | flops | bytes accessed | tf_op | source)
XLA Modules:
  0.0 451.5 jit_solution(15347395934908366569)
XLA Ops:
  7.2 0.0 all-gather.3.cloned.1.call-start
  7.2 1.1 constant_dynamic-slice_fusion
  8.3 0.9 constant_dynamic-slice_fusion.1
  9.3 0.9 pad_maximum_fusion.1
  10.2 0.0 reduce-scatter.3.cloned.1.call-start
  10.3 1.9 gather_fusion
  12.2 69.2 %all-gather.3.cloned.1.call-done = bf16[2816,2048]{1,0:T(8,128)(2,1)} async-done(((bf16[176,2048]{1,0:T(8,128)(2,1)}), bf16[2816,2048]{1,0:T(8,128)(2,1)}) %all-gather.3.cloned.1.call-update) | async-done | bytes 11534352 | tf_op jit(solution)/shard_map/all_gather | solution.py:95
  81.5 2.1 slice.50
  83.6 8.3 %slice.51 = bf16[8,2,128,2048]{3,2,0,1:T(8,128)(2,1)} slice(bf16[8,2,176,2048]{3,2,0,1:T(8,128)(2,1)} %bitcast.55), slice={[0:8], [0:2], [48:176], [0:2048]} | slice | bytes 16777216 | tf_op jit(solution)/shard_map/slice | solution.py:98
  91.9 0.4 copy.34
  92.3 8.3 %copy.35 = bf16[8,2,128,2048]{3,2,1,0:T(8,128)(2,1)} copy(bf16[8,2,128,2048]{3,2,0,1:T(8,128)(2,1)} %slice.51) | data formatting | bytes 16777216 | tf_op jit(solution)/shard_map/slice | solution.py:98
  100.6 1.1 convolution_multiply_fusion.1
  101.7 6.8 %multiply_reduce_fusion.1 = (f32[256]{0:T(256)S(1)}, f32[256,2048]{1,0:T(8,128)S(1)}) fusion(bf16[2048,2048]{1,0:T(8,128)(2,1)} %bitcast.56, f32[256,2048]{1,0:T(8,128)S(1)} %convolution_multiply_fusion.1), kind=kOutput, calls=%fused_computation.27 | convolution fusion | flops 2153774848 | bytes 12583936 | tf_op jit(solution)/shard_map/dot_general | solution.py:123
  108.6 0.6 convolution_multiply_fusion.3
  109.1 0.1 copy.36
  109.3 0.1 fusion.35
  109.4 0.2 fusion.36
  109.6 0.8 multiply_reduce_fusion
  110.4 1.5 multiply_convert_fusion.2
  111.9 10.1 %multiply_convert_fusion.1 = bf16[768,2048]{1,0:T(8,128)(2,1)} fusion(f32[256,2048]{1,0:T(8,128)} %copy-done.6, bf16[256,2048]{1,0:T(8,128)(2,1)} %multiply_convert_fusion.2, bf16[2048,2048]{1,0:T(8,128)(2,1)} %bitcast.57, bf16[256,768]{1,0:T(8,128)(2,1)S(1)} %copy-done.10, pred[256]{0:T(512)(128)(4,1)S(1)} %compare_and_fusion), kind=kOutput, calls=%fused_computation.2 | convolution fusion | flops 2967142400 | bytes 15073536 | tf_op jit(solution)/shard_map/dot_general | solution.py:139
  122.1 0.2 reduce-scatter.5.cloned.1.call-start
  122.3 1.3 copy-done.7
  123.6 0.3 copy-done.12
  123.9 6.2 %multiply_convert_fusion = bf16[2048,2048]{1,0:T(8,128)(2,1)} fusion(bf16[256,2048]{1,0:T(8,128)(2,1)S(1)} %copy-done.12, f32[256,2048]{1,0:T(8,128)S(1)} %copy-done.7), kind=kOutput, calls=%fused_computation.1 | convolution fusion | flops 2160590848 | bytes 11534336 | tf_op jit(solution)/shard_map/dot_general | solution.py:126
  130.2 34.8 %reduce-scatter.3.cloned.1.call-done = bf16[96,2048]{1,0:T(8,128)(2,1)} async-done(((bf16[768,2048]{1,0:T(8,128)(2,1)}), bf16[96,2048]{1,0:T(8,128)(2,1)}) %reduce-scatter.3.cloned.1.call-update) | async-done | bytes 393232 | tf_op jit(solution)/shard_map/reduce_scatter | solution.py:138
  165.0 2.5 fusion.24
  167.5 95.4 %reduce-scatter.5.cloned.1.call-done = bf16[256,2048]{1,0:T(8,128)(2,1)} async-done(((bf16[2048,2048]{1,0:T(8,128)(2,1)}), bf16[256,2048]{1,0:T(8,128)(2,1)}) %reduce-scatter.5.cloned.1.call-update) | async-done | bytes 1048592 | tf_op jit(solution)/shard_map/reduce_scatter | solution.py:125
  263.0 3.2 fusion.3
  266.2 0.3 pad_maximum_fusion
  266.5 2.3 copy.37
  268.9 10.2 %all-to-all-start = ((f32[352,32,64]{0,2,1:T(8,128)}), f32[352,32,64]{0,2,1:T(8,128)S(1)}, u32[]{:S(2)}, u32[]{:S(2)}) async-start(f32[352,32,64]{0,2,1:T(8,128)} %bitcast.50), calls=%async_computation.2 | async-start | bytes 6291456 | tf_op jit(solution)/shard_map/all_to_all | solution.py:69
  279.1 2.3 copy.33
  281.4 2.0 copy.32
  283.4 2.3 copy.39
  285.6 2.0 copy.38
  287.6 62.7 %all-to-all-done = f32[352,32,64]{0,2,1:T(8,128)S(1)} async-done(((f32[352,32,64]{0,2,1:T(8,128)}), f32[352,32,64]{0,2,1:T(8,128)S(1)}, u32[]{:S(2)}, u32[]{:S(2)}) %all-to-all-start) | async-done | bytes 2883616 | tf_op jit(solution)/shard_map/all_to_all | solution.py:69
  350.4 0.2 reduce_sum.39
  350.5 0.9 subtract_convert_fusion
  351.5 0.1 copy.40
  351.6 0.4 broadcast_in_dim.30
  352.0 80.2 %all_to_all.18 = bf16[32,352,128]{2,1,0:T(8,128)(2,1)} all-to-all(bf16[32,352,128]{2,1,0:T(8,128)(2,1)S(1)} %broadcast_in_dim.30), channel_id=1, replica_groups=mesh['zh'=2,'y'=4,'x'=4,'zl'=4,'c'=2] {'zh','y','x'}, dimensions={0} | all-to-all | bytes 5767168 | tf_op jit(solution)/shard_map/all_to_all | solution.py:77
  432.3 3.4 copy.41
  435.6 2.4 fusion.60
  438.0 1.2 fusion.61
  439.2 2.4 copy.43
  441.6 1.4 copy.45
  443.1 1.0 copy.42
  444.0 1.0 copy.44
  (41 shorter events, 0.2 us)
Async XLA Ops:
  7.2 3.1 copy-start
  7.2 3.1 copy-start.15
  7.2 74.3 %all-gather.3.cloned.1.call-start = ((), (), s32[]{:S(2)}) async-start(), calls=%async_computation.6 | async-start | bytes 12255232 | tf_op jit(solution)/shard_map/all_gather | solution.py:95
  10.2 154.8 %reduce-scatter.3.cloned.1.call-start = ((), (), s32[]{:S(2)}) async-start(), calls=%async_computation.4 | async-start | bytes 3538944 | tf_op jit(solution)/shard_map/reduce_scatter | solution.py:138
  92.3 8.3 %copy-start.10 = (bf16[256,768]{1,0:T(8,128)(2,1)S(1)}, bf16[256,768]{1,0:T(8,128)(2,1)}, u32[]{:S(2)}) copy-start(bf16[256,768]{1,0:T(8,128)(2,1)} %gather_fusion) | copy-start | bytes 1179652
  101.7 6.8 %copy-start.6 = (f32[256,2048]{1,0:T(8,128)}, f32[256,2048]{1,0:T(8,128)S(1)}, u32[]{:S(2)}) copy-start(f32[256,2048]{1,0:T(8,128)S(1)} %convolution_multiply_fusion.1) | copy-start | bytes 6291460
  108.6 1.0 copy-start.16
  122.0 1.6 copy-start.7
  122.0 1.9 copy-start.12
  122.1 140.9 %reduce-scatter.5.cloned.1.call-start = ((), (), s32[]{:S(2)}) async-start(), calls=%async_computation.5 | async-start | bytes 9437184 | tf_op jit(solution)/shard_map/reduce_scatter | solution.py:125
  130.1 34.9 %copy-start.5 = (bf16[96,2048]{1,0:T(8,128)(2,1)S(1)}, bf16[96,2048]{1,0:T(8,128)(2,1)}, u32[]{:S(2)}) copy-start(bf16[96,2048]{1,0:T(8,128)(2,1)} %param.14) | copy-start | bytes 1179652
  130.1 34.9 %copy-start.13 = (bf16[1,96,2048]{2,1,0:T(8,128)(2,1)S(1)}, bf16[1,96,2048]{2,1,0:T(8,128)(2,1)}, u32[]{:S(2)}) copy-start(bf16[1,96,2048]{2,1,0:T(8,128)(2,1)} %param.18) | copy-start | bytes 1179652
  130.1 34.9 %copy-start.14 = (bf16[1,96,2048]{2,1,0:T(8,128)(2,1)S(1)}, bf16[1,96,2048]{2,1,0:T(8,128)(2,1)}, u32[]{:S(2)}) copy-start(bf16[1,96,2048]{2,1,0:T(8,128)(2,1)} %param.16) | copy-start | bytes 1179652
  130.2 132.8 %copy-start.2 = (bf16[256,2048]{1,0:T(8,128)(2,1)S(1)}, bf16[256,2048]{1,0:T(8,128)(2,1)}, u32[]{:S(2)}) copy-start(bf16[256,2048]{1,0:T(8,128)(2,1)} %param.15) | copy-start | bytes 3145732
  130.2 132.8 %copy-start.11 = (bf16[1,256,2048]{2,1,0:T(8,128)(2,1)S(1)}, bf16[1,256,2048]{2,1,0:T(8,128)(2,1)}, u32[]{:S(2)}) copy-start(bf16[1,256,2048]{2,1,0:T(8,128)(2,1)} %param.19) | copy-start | bytes 3145732
  263.0 3.2 copy-start.4
  268.9 81.5 %all-to-all-start = ((f32[352,32,64]{0,2,1:T(8,128)}), f32[352,32,64]{0,2,1:T(8,128)S(1)}, u32[]{:S(2)}, u32[]{:S(2)}) async-start(f32[352,32,64]{0,2,1:T(8,128)} %bitcast.50), calls=%async_computation.2 | async-start | bytes 6291456 | tf_op jit(solution)/shard_map/all_to_all | solution.py:69
  439.2 2.4 copy-start.3
  439.2 3.8 copy-start.9
  439.2 4.8 %copy-start.8 = (bf16[1,96,32,64]{1,3,0,2:T(8,128)(2,1)S(1)}, bf16[1,96,32,64]{1,3,0,2:T(8,128)(2,1)}, u32[]{:S(2)}) copy-start(bf16[1,96,32,64]{1,3,0,2:T(8,128)(2,1)} %get-tuple-element.20) | copy-start | bytes 1179652
  439.2 5.8 %copy-start.1 = (bf16[1,128,768]{2,1,0:T(8,128)(2,1)S(1)}, bf16[1,128,768]{2,1,0:T(8,128)(2,1)}, u32[]{:S(2)}) copy-start(bf16[1,128,768]{2,1,0:T(8,128)(2,1)} %param.11) | copy-start | bytes 589828
Sparse Core Ops, SparseCore 0:
  10.4 71.0 all-gather.2
  122.2 42.7 reduce-scatter.2
  167.6 95.3 reduce-scatter.4

commit v4 on v3

--- a/solution.py
+++ b/solution.py
@@ -63,19 +63,26 @@
 
 
 def wide_mean_update(delta, momentum, weights):
-    sites = lax.axis_size(WIDE)
+    plane = ("y", "x")
+    n_plane = lax.axis_size(plane)
+    n_half = lax.axis_size("zh")
+    sites = n_plane * n_half
     rows, cols = delta.shape
-    piece = cols // sites
-    got = lax.all_to_all(delta, WIDE, 1, 0, tiled=True)
-    mean = jnp.sum(got.reshape(sites, rows, piece), axis=0) / sites
-    start = lax.axis_index(WIDE) * piece
-    mom_piece = lax.dynamic_slice_in_dim(momentum, start, piece, axis=1)
-    w_piece = lax.dynamic_slice_in_dim(weights, start, piece, axis=1)
+    p1 = cols // n_plane
+    p2 = p1 // n_half
+    got = lax.all_to_all(delta, plane, 1, 0, tiled=True)
+    part = jnp.sum(got.reshape(n_plane, rows, p1), axis=0)
+    got = lax.all_to_all(part, "zh", 1, 0, tiled=True)
+    mean = jnp.sum(got.reshape(n_half, rows, p2), axis=0) / sites
+    start = lax.axis_index(plane) * p1 + lax.axis_index("zh") * p2
+    mom_piece = lax.dynamic_slice_in_dim(momentum, start, p2, axis=1)
+    w_piece = lax.dynamic_slice_in_dim(weights, start, p2, axis=1)
     new_piece, vel_piece = outer_update(mean, mom_piece, w_piece)
-    both = jnp.concatenate([new_piece, vel_piece], axis=1)
-    spread = jnp.broadcast_to(both[None], (sites,) + both.shape)
-    back = lax.all_to_all(spread, WIDE, 0, 0, tiled=True)
-    back = back.reshape(sites, rows, 2, piece).transpose(2, 1, 0, 3).reshape(2, rows, cols)
+    both = jnp.stack([new_piece, vel_piece], axis=0)
+    back = lax.all_to_all(jnp.broadcast_to(both[None], (n_half,) + both.shape), "zh", 0, 0, tiled=True)
+    back = back.transpose(1, 2, 0, 3).reshape(2, rows, p1)
+    back = lax.all_to_all(jnp.broadcast_to(back[None], (n_plane,) + back.shape), plane, 0, 0, tiled=True)
+    back = back.transpose(1, 2, 0, 3).reshape(2, rows, cols)
     return back[0], back[1]
 
 

time: 456 us -> 401 us (0.88)
  waiting for transfers between devices: 262 us -> 205 us
  blocking collectives: 80.2 us -> 94.8 us
  starting transfers between devices: 10.5 us -> 4.4 us
  local copies, waits for them, and re-layouts: 48.9 us -> 43.7 us
    all_to_all x1, waiting for transfers between devices: 62.7 us -> 5.03 us  [wide_mean_update(): got = lax.all_to_all(part, 'zh', 1, 0, tiled=True)]
    all_to_all x1 -> x3, blocking collectives: 80.2 us -> 94.8 us  [the longest x1 44.7 us: wide_mean_update(): got = lax.all_to_all(delta, plane, 1, 0, tiled=True)]
    all_to_all x1, starting transfers between devices: 10.2 us -> 4.1 us  [wide_mean_update(): got = lax.all_to_all(part, 'zh', 1, 0, tiled=True)]
    unnamed x42 -> x34, local copies, waits for them, and re-layouts: 15.9 us -> 9.99 us
where the time goes in v4:
time: 401 us; the launch traced here: 397 us
  waiting for transfers between devices  205 us (51%)
  blocking collectives  94.8 us (24%)
  local copies, waits for them, and re-layouts  43.7 us (11%)
  matrix products  25.6 us (6%)
  between operations  14 us (3%)
  other arithmetic  9.34 us (2%)
  starting transfers between devices  4.4 us (1%)
    reduce_scatter x1, waiting for transfers between devices, shards(): lax.psum_scatter((scale_two * jnp.dot(active.T, embed_half, preferred_ele...  96.1 us
    all_gather x1, waiting for transfers between devices, gather_weights(): got = lax.all_gather(mine, ('zh',) + NARROW, axis=0, tiled=False)  69.2 us
    all_to_all x1, blocking collectives, wide_mean_update(): got = lax.all_to_all(delta, plane, 1, 0, tiled=True)  44.7 us
    all_to_all x1, blocking collectives, wide_mean_update(): lax.all_to_all(jnp.broadcast_to(back[None], (n_plane,) + back.shape), pla...  38.7 us
    reduce_scatter x1, waiting for transfers between devices, shards(): lax.psum_scatter((scale_one * jnp.dot(inputs.T, hidden_half, preferred_el...  34.8 us
    slice x2, local copies, waits for them, and re-layouts, gather_weights(): second = got[:, :, r1:].reshape(shards_n * halves * r2, -1)  16.7 us
    all_to_all x1, blocking collectives, wide_mean_update(): lax.all_to_all(jnp.broadcast_to(both[None], (n_half,) + both.shape), 'zh'...  11.4 us
    dot_general x1, matrix products, shards(): jnp.dot(inputs.T, hidden_half, preferred_element_type=jnp.float32)  10.2 us
  transfers between devices with their start and end apart: 4, of which 4 were waited for; matrix products, arithmetic and copies ran while one was open for 4% of the time, Pallas kernels for 0%

profile of v4, /device:TPU:64, one launch (start us, length us, event | category | flops | bytes accessed | tf_op | source)
XLA Modules:
  0.0 397.1 jit_solution(6609158045635494583)
XLA Ops:
  7.2 1.1 constant_dynamic-slice_fusion
  8.3 0.9 constant_dynamic-slice_fusion.1
  9.3 0.9 pad_maximum_fusion
  10.3 1.9 gather_fusion
  12.2 69.2 %all-gather.3.cloned.1.call-done = bf16[2816,2048]{1,0:T(8,128)(2,1)} async-done(((bf16[176,2048]{1,0:T(8,128)(2,1)}), bf16[2816,2048]{1,0:T(8,128)(2,1)}) %all-gather.3.cloned.1.call-update) | async-done | bytes 11534352 | tf_op jit(solution)/shard_map/all_gather | solution.py:102
  81.5 2.1 slice.50
  83.6 8.3 %slice.51 = bf16[8,2,128,2048]{3,2,0,1:T(8,128)(2,1)} slice(bf16[8,2,176,2048]{3,2,0,1:T(8,128)(2,1)} %bitcast.63), slice={[0:8], [0:2], [48:176], [0:2048]} | slice | bytes 16777216 | tf_op jit(solution)/shard_map/slice | solution.py:105
  91.9 0.4 copy.38
  92.3 8.3 %copy.39 = bf16[8,2,128,2048]{3,2,1,0:T(8,128)(2,1)} copy(bf16[8,2,128,2048]{3,2,0,1:T(8,128)(2,1)} %slice.51) | data formatting | bytes 16777216 | tf_op jit(solution)/shard_map/slice | solution.py:105
  100.7 1.1 convolution_multiply_fusion.1
  101.8 6.8 %multiply_reduce_fusion.1 = (f32[256]{0:T(256)S(1)}, f32[256,2048]{1,0:T(8,128)S(1)}) fusion(bf16[2048,2048]{1,0:T(8,128)(2,1)} %bitcast.64, f32[256,2048]{1,0:T(8,128)S(1)} %convolution_multiply_fusion.1), kind=kOutput, calls=%fused_computation.28 | convolution fusion | flops 2153774848 | bytes 12583936 | tf_op jit(solution)/shard_map/dot_general | solution.py:130
  108.6 0.6 convolution_multiply_fusion.3
  109.2 0.1 copy.40
  109.4 0.2 fusion.36
  109.6 0.8 multiply_reduce_fusion
  110.4 1.5 multiply_convert_fusion.2
  111.9 10.2 %multiply_convert_fusion.1 = bf16[768,2048]{1,0:T(8,128)(2,1)} fusion(f32[256,2048]{1,0:T(8,128)} %copy-done.5, bf16[256,2048]{1,0:T(8,128)(2,1)} %multiply_convert_fusion.2, bf16[2048,2048]{1,0:T(8,128)(2,1)} %bitcast.65, bf16[256,768]{1,0:T(8,128)(2,1)S(1)} %copy-done.9, pred[256]{0:T(512)(128)(4,1)S(1)} %compare_and_fusion), kind=kOutput, calls=%fused_computation.2 | convolution fusion | flops 2967142400 | bytes 15073536 | tf_op jit(solution)/shard_map/dot_general | solution.py:146
  122.1 0.2 reduce-scatter.5.cloned.1.call-start
  122.3 1.3 copy-done.6
  123.7 0.3 copy-done.11
  123.9 6.2 %multiply_convert_fusion = bf16[2048,2048]{1,0:T(8,128)(2,1)} fusion(bf16[256,2048]{1,0:T(8,128)(2,1)S(1)} %copy-done.11, f32[256,2048]{1,0:T(8,128)S(1)} %copy-done.6), kind=kOutput, calls=%fused_computation.1 | convolution fusion | flops 2160590848 | bytes 11534336 | tf_op jit(solution)/shard_map/dot_general | solution.py:133
  130.2 34.8 %reduce-scatter.3.cloned.1.call-done = bf16[96,2048]{1,0:T(8,128)(2,1)} async-done(((bf16[768,2048]{1,0:T(8,128)(2,1)}), bf16[96,2048]{1,0:T(8,128)(2,1)}) %reduce-scatter.3.cloned.1.call-update) | async-done | bytes 393232 | tf_op jit(solution)/shard_map/reduce_scatter | solution.py:145
  165.1 1.9 fusion.24
  166.9 96.1 %reduce-scatter.5.cloned.1.call-done = bf16[256,2048]{1,0:T(8,128)(2,1)} async-done(((bf16[2048,2048]{1,0:T(8,128)(2,1)}), bf16[256,2048]{1,0:T(8,128)(2,1)}) %reduce-scatter.5.cloned.1.call-update) | async-done | bytes 1048592 | tf_op jit(solution)/shard_map/reduce_scatter | solution.py:132
  263.1 3.2 fusion.3
  266.2 0.3 copy_bitcast_fusion
  266.5 44.7 %all_to_all.36 = f32[352,16,128]{2,0,1:T(8,128)S(1)} all-to-all(f32[352,16,128]{2,0,1:T(8,128)S(1)} %copy_bitcast_fusion), channel_id=1, replica_groups=mesh['zh'=2,'y'=4,'x'=4,'zl'=4,'c'=2] {'y','x'}, dimensions={1} | all-to-all | bytes 5767168 | tf_op jit(solution)/shard_map/all_to_all | solution.py:73
  311.2 0.1 reduce_sum.48
  311.4 0.8 copy.43
  312.2 4.1 %all-to-all-start.1 = ((f32[352,2,64]{0,2,1:T(8,128)}), f32[352,2,64]{0,2,1:T(8,128)}, u32[]{:S(2)}, u32[]{:S(2)}) async-start(f32[352,2,64]{0,2,1:T(8,128)} %bitcast.15), calls=%async_computation.3 | async-start | bytes 393216 | tf_op jit(solution)/shard_map/all_to_all | solution.py:75
  316.3 1.5 copy.37
  317.8 0.3 copy.36
  318.0 1.5 copy.45
  319.5 1.3 copy.44
  320.8 5.0 %all-to-all-done.1 = f32[352,2,64]{0,2,1:T(8,128)} async-done(((f32[352,2,64]{0,2,1:T(8,128)}), f32[352,2,64]{0,2,1:T(8,128)}, u32[]{:S(2)}, u32[]{:S(2)}) %all-to-all-start.1) | async-done | bytes 180256 | tf_op jit(solution)/shard_map/all_to_all | solution.py:75
  325.8 1.0 reduce_sum.49
  326.8 0.1 fusion.49
  327.0 11.4 %all_to_all.37 = bf16[2,2,352,64]{2,3,1,0:T(8,128)(2,1)S(1)} all-to-all(bf16[2,2,352,64]{2,3,1,0:T(8,128)(2,1)S(1)} %broadcast_in_dim.37), channel_id=1, replica_groups=mesh['zh'=2,'y'=4,'x'=4,'zl'=4,'c'=2] {'zh'}, dimensions={0} | all-to-all | bytes 360448 | tf_op jit(solution)/shard_map/all_to_all | solution.py:82
  338.4 0.2 copy.47
  338.6 0.6 broadcast_in_dim.39
  339.1 38.7 %all_to_all.38 = bf16[16,2,352,128]{3,2,1,0:T(8,128)(2,1)} all-to-all(bf16[16,2,352,128]{3,2,1,0:T(8,128)(2,1)S(1)} %broadcast_in_dim.39), channel_id=1, replica_groups=mesh['zh'=2,'y'=4,'x'=4,'zl'=4,'c'=2] {'y','x'}, dimensions={0} | all-to-all | bytes 5767168 | tf_op jit(solution)/shard_map/all_to_all | solution.py:84
  377.9 3.4 copy.48
  381.3 2.3 fusion.62
  383.6 1.2 fusion.63
  384.9 2.4 copy.51
  387.3 1.4 copy.52
  388.7 1.0 copy.53
  389.6 1.0 copy.54
  (40 shorter events, 0.4 us)
Async XLA Ops:
  7.2 3.1 copy-start
  7.2 3.1 copy-start.12
  7.2 74.3 %all-gather.3.cloned.1.call-start = ((), (), s32[]{:S(2)}) async-start(), calls=%async_computation.8 | async-start | bytes 12255232 | tf_op jit(solution)/shard_map/all_gather | solution.py:102
  10.2 154.9 %reduce-scatter.3.cloned.1.call-start = ((), (), s32[]{:S(2)}) async-start(), calls=%async_computation.6 | async-start | bytes 3538944 | tf_op jit(solution)/shard_map/reduce_scatter | solution.py:145
  92.3 8.3 %copy-start.9 = (bf16[256,768]{1,0:T(8,128)(2,1)S(1)}, bf16[256,768]{1,0:T(8,128)(2,1)}, u32[]{:S(2)}) copy-start(bf16[256,768]{1,0:T(8,128)(2,1)} %gather_fusion) | copy-start | bytes 1179652
  101.7 6.8 %copy-start.5 = (f32[256,2048]{1,0:T(8,128)}, f32[256,2048]{1,0:T(8,128)S(1)}, u32[]{:S(2)}) copy-start(f32[256,2048]{1,0:T(8,128)S(1)} %convolution_multiply_fusion.1) | copy-start | bytes 6291460
  108.6 1.0 copy-start.13
  122.1 1.6 copy-start.6
  122.1 1.9 copy-start.11
  122.1 140.9 %reduce-scatter.5.cloned.1.call-start = ((), (), s32[]{:S(2)}) async-start(), calls=%async_computation.7 | async-start | bytes 9437184 | tf_op jit(solution)/shard_map/reduce_scatter | solution.py:132
  130.2 34.9 %copy-start.4 = (bf16[96,2048]{1,0:T(8,128)(2,1)S(1)}, bf16[96,2048]{1,0:T(8,128)(2,1)}, u32[]{:S(2)}) copy-start(bf16[96,2048]{1,0:T(8,128)(2,1)} %param.14) | copy-start | bytes 1179652
  130.2 132.8 %copy-start.2 = (bf16[256,2048]{1,0:T(8,128)(2,1)S(1)}, bf16[256,2048]{1,0:T(8,128)(2,1)}, u32[]{:S(2)}) copy-start(bf16[256,2048]{1,0:T(8,128)(2,1)} %param.15) | copy-start | bytes 3145732
  130.2 132.8 %copy-start.10 = (bf16[1,256,2048]{2,1,0:T(8,128)(2,1)S(1)}, bf16[1,256,2048]{2,1,0:T(8,128)(2,1)}, u32[]{:S(2)}) copy-start(bf16[1,256,2048]{2,1,0:T(8,128)(2,1)} %param.19) | copy-start | bytes 3145732
  312.2 13.7 %all-to-all-start.1 = ((f32[352,2,64]{0,2,1:T(8,128)}), f32[352,2,64]{0,2,1:T(8,128)}, u32[]{:S(2)}, u32[]{:S(2)}) async-start(f32[352,2,64]{0,2,1:T(8,128)} %bitcast.15), calls=%async_computation.3 | async-start | bytes 393216 | tf_op jit(solution)/shard_map/all_to_all | solution.py:75
  384.8 2.4 copy-start.3
  384.8 3.8 copy-start.8
  384.8 4.8 %copy-start.7 = (bf16[1,96,16,128]{1,3,2,0:T(8,128)(2,1)S(1)}, bf16[1,96,16,128]{1,3,2,0:T(8,128)(2,1)}, u32[]{:S(2)}) copy-start(bf16[1,96,16,128]{1,3,2,0:T(8,128)(2,1)} %get-tuple-element.12) | copy-start | bytes 1179652
  384.9 5.8 %copy-start.1 = (bf16[1,128,768]{2,1,0:T(8,128)(2,1)S(1)}, bf16[1,128,768]{2,1,0:T(8,128)(2,1)}, u32[]{:S(2)}) copy-start(bf16[1,128,768]{2,1,0:T(8,128)(2,1)} %param.11) | copy-start | bytes 589828
Sparse Core Ops, SparseCore 0:
  10.4 71.0 all-gather.2
  122.2 42.7 reduce-scatter.2
  167.6 95.3 reduce-scatter.4

commit v5 on v4

--- a/solution.py
+++ b/solution.py
@@ -137,27 +137,22 @@
         scatter_dimension=0,
         tiled=True,
     ).astype(jnp.float32)
-    delta_second = adam_delta(grad_second, m_second[0], v_second[0], w_second)
     active_grad = scale_two * jnp.dot(
         embed_half, second_whole.T, preferred_element_type=jnp.float32
     )
     hidden_half = gelu_back(active_grad)[0].astype(jnp.bfloat16)
+    term_first = (
+        scale_one * jnp.dot(inputs.T, hidden_half, preferred_element_type=jnp.float32)
+    ).astype(jnp.bfloat16)
+    term_first, grad_second = lax.optimization_barrier((term_first, grad_second))
+    delta_second = adam_delta(grad_second, m_second[0], v_second[0], w_second)
+    new_second, vel_second = wide_mean_update(delta_second, mom_second, w_second)
     grad_first = lax.psum_scatter(
-        (scale_one * jnp.dot(inputs.T, hidden_half, preferred_element_type=jnp.float32)).astype(
-            jnp.bfloat16
-        ),
-        NARROW,
-        scatter_dimension=0,
-        tiled=True,
+        term_first, NARROW, scatter_dimension=0, tiled=True
     ).astype(jnp.float32)
     delta_first = adam_delta(grad_first, m_first[0], v_first[0], w_first)
-    rows_first = delta_first.shape[0]
-    new_w, vel = wide_mean_update(
-        jnp.concatenate([delta_first, delta_second], axis=0),
-        jnp.concatenate([mom_first, mom_second], axis=0),
-        jnp.concatenate([w_first, w_second], axis=0),
-    )
-    return (new_w[:rows_first], new_w[rows_first:], vel[:rows_first], vel[rows_first:])
+    new_first, vel_first = wide_mean_update(delta_first, mom_first, w_first)
+    return (new_first, new_second, vel_first, vel_second)
 
 
 def solution(mesh):

time: 401 us -> 387 us (0.965)
  blocking collectives: 94.8 us -> 36.2 us
  starting transfers between devices: 4.4 us -> 26.6 us
  waiting for transfers between devices: 205 us -> 221 us
  local copies, waits for them, and re-layouts: 43.7 us -> 48.4 us
    all_to_all x0 -> x5, waiting for transfers between devices: none -> 55.5 us  [the longest x2 29.6 us: wide_mean_update(): lax.all_to_all(jnp.broadcast_to(back[None], (n_plane,) + back.shape), pla...]
    all_to_all x2 -> x0, blocking collectives: 50.1 us -> none  [the longest x1 38.7 us: wide_mean_update(): lax.all_to_all(jnp.broadcast_to(back[None], (n_plane,) + back.shape), pla...]
    reduce_scatter x1, waiting for transfers between devices: 34.8 us -> 0.01 us  [shards(): lax.psum_scatter(term_first, NARROW, scatter_dimension=0, tiled=True)]
    all_to_all x0 -> x5, starting transfers between devices: none -> 18.3 us  [the longest x2 8 us: wide_mean_update(): lax.all_to_all(jnp.broadcast_to(back[None], (n_plane,) + back.shape), pla...]
    reduce_scatter x1, waiting for transfers between devices: 96.1 us -> 81.5 us  [shards(): lax.psum_scatter((scale_two * jnp.dot(active.T, embed_half, preferred_ele...]
    all_to_all x1 -> x2, waiting for transfers between devices: 5.03 us -> 13.8 us  [wide_mean_update(): got = lax.all_to_all(part, 'zh', 1, 0, tiled=True)]
    all_to_all x1, blocking collectives: 44.7 us -> 36.2 us  [wide_mean_update(): got = lax.all_to_all(delta, plane, 1, 0, tiled=True)]
    all_to_all x1 -> x2, other arithmetic: 0.29 us -> 6.15 us  [wide_mean_update(): got = lax.all_to_all(delta, plane, 1, 0, tiled=True)]
  transfers between devices with their start and end apart: 4 -> 10, of which waited for: 4 -> 9; matrix products, arithmetic and copies ran while one was open for 4% -> 8% of each run, Pallas kernels for 0% -> 0%
where the time goes in v5:
time: 387 us; the launch traced here: 383 us
  waiting for transfers between devices  221 us (57%)
  local copies, waits for them, and re-layouts  48.4 us (13%)
  blocking collectives  36.2 us (9%)
  starting transfers between devices  26.6 us (7%)
  matrix products  26.6 us (7%)
  between operations  14.1 us (4%)
  other arithmetic  10.3 us (3%)
    reduce_scatter x1, waiting for transfers between devices, shards(): lax.psum_scatter((scale_two * jnp.dot(active.T, embed_half, preferred_ele...  81.5 us
    all_gather x1, waiting for transfers between devices, gather_weights(): got = lax.all_gather(mine, ('zh',) + NARROW, axis=0, tiled=False)  69.9 us
    all_to_all x1, blocking collectives, wide_mean_update(): got = lax.all_to_all(delta, plane, 1, 0, tiled=True)  36.2 us
    all_to_all x2, waiting for transfers between devices, wide_mean_update(): lax.all_to_all(jnp.broadcast_to(back[None], (n_plane,) + back.shape), pla...  29.6 us
    slice x2, local copies, waits for them, and re-layouts, gather_weights(): second = got[:, :, r1:].reshape(shards_n * halves * r2, -1)  16.6 us
    all_to_all x2, waiting for transfers between devices, wide_mean_update(): lax.all_to_all(jnp.broadcast_to(both[None], (n_half,) + both.shape), 'zh'...  16.2 us
    all_to_all x2, waiting for transfers between devices, wide_mean_update(): got = lax.all_to_all(part, 'zh', 1, 0, tiled=True)  13.8 us
    all_to_all x1, waiting for transfers between devices, wide_mean_update(): got = lax.all_to_all(delta, plane, 1, 0, tiled=True)  9.8 us
  transfers between devices with their start and end apart: 10, of which 9 were waited for; matrix products, arithmetic and copies ran while one was open for 8% of the time, Pallas kernels for 0%

profile of v5, /device:TPU:64, one launch (start us, length us, event | category | flops | bytes accessed | tf_op | source)
XLA Modules:
  0.0 383.0 jit_solution(6880617024968860137)
XLA Ops:
  7.3 1.2 constant_dynamic-slice_fusion.3
  8.4 0.9 constant_dynamic-slice_fusion.4
  9.4 0.9 pad_maximum_fusion
  10.4 1.2 gather_fusion
  11.6 69.9 %all-gather.3.cloned.1.call-done = bf16[2816,2048]{1,0:T(8,128)(2,1)} async-done(((bf16[176,2048]{1,0:T(8,128)(2,1)}), bf16[2816,2048]{1,0:T(8,128)(2,1)}) %all-gather.3.cloned.1.call-update) | async-done | bytes 11534352 | tf_op jit(solution)/shard_map/all_gather | solution.py:102
  81.5 4.0 %slice.30 = bf16[8,2,48,2048]{3,2,0,1:T(8,128)(2,1)} slice(bf16[8,2,176,2048]{3,2,0,1:T(8,128)(2,1)} %bitcast.90), slice={[0:8], [0:2], [0:48], [0:2048]} | slice | bytes 6291456 | tf_op jit(solution)/shard_map/slice | solution.py:104
  85.5 8.3 %slice.31 = bf16[8,2,128,2048]{3,2,0,1:T(8,128)(2,1)} slice(bf16[8,2,176,2048]{3,2,0,1:T(8,128)(2,1)} %bitcast.91), slice={[0:8], [0:2], [48:176], [0:2048]} | slice | bytes 16777216 | tf_op jit(solution)/shard_map/slice | solution.py:105
  93.8 2.1 copy.46
  95.9 8.3 %copy.47 = bf16[8,2,128,2048]{3,2,1,0:T(8,128)(2,1)} copy(bf16[8,2,128,2048]{3,2,0,1:T(8,128)(2,1)} %slice.31) | data formatting | bytes 16777216 | tf_op jit(solution)/shard_map/slice | solution.py:105
  104.2 1.1 convolution_multiply_fusion.1
  105.2 6.8 %multiply_reduce_fusion.1 = (f32[256]{0:T(256)S(1)}, f32[256,2048]{1,0:T(8,128)S(1)}) fusion(bf16[2048,2048]{1,0:T(8,128)(2,1)} %bitcast.92, f32[256,2048]{1,0:T(8,128)S(1)} %convolution_multiply_fusion.1), kind=kOutput, calls=%fused_computation.26 | convolution fusion | flops 2153774848 | bytes 12583936 | tf_op jit(solution)/shard_map/dot_general | solution.py:130
  112.1 1.3 convolution_multiply_fusion.3
  113.4 1.1 copy.48
  114.8 1.7 multiply_reduce_fusion
  117.0 1.0 copy-done.7
  118.2 6.2 %multiply_convert_fusion = bf16[2048,2048]{1,0:T(8,128)(2,1)} fusion(bf16[256,2048]{1,0:T(8,128)(2,1)S(1)} %multiply_convert_fusion.2, f32[256,2048]{1,0:T(8,128)S(1)} %copy-done.3), kind=kOutput, calls=%fused_computation.1 | convolution fusion | flops 2160590848 | bytes 11534336 | tf_op jit(solution)/shard_map/dot_general | solution.py:133
  124.7 1.3 copy-done.4
  126.1 9.5 %multiply_convert_fusion.1 = bf16[768,2048]{1,0:T(8,128)(2,1)} fusion(f32[256,2048]{1,0:T(8,128)S(1)} %copy-done.4, bf16[256,2048]{1,0:T(8,128)(2,1)} %copy-done.7, bf16[2048,2048]{1,0:T(8,128)(2,1)} %bitcast.93, bf16[256,768]{1,0:T(8,128)(2,1)S(1)} %copy-done.6, pred[256]{0:T(512)(128)(4,1)S(1)} %compare_and_fusion), kind=kOutput, calls=%fused_computation.2 | convolution fusion | flops 2967142400 | bytes 15073536 | tf_op jit(solution)/shard_map/dot_general | solution.py:145
  135.6 81.5 %reduce-scatter.3.cloned.1.call-done = bf16[256,2048]{1,0:T(8,128)(2,1)} async-done(((bf16[2048,2048]{1,0:T(8,128)(2,1)}), bf16[256,2048]{1,0:T(8,128)(2,1)}) %reduce-scatter.3.cloned.1.call-update) | async-done | bytes 1048592 | tf_op jit(solution)/shard_map/reduce_scatter | solution.py:132
  217.1 1.5 convert_element_type.90
  218.6 3.4 copy_bitcast_fusion
  222.0 36.2 %all_to_all.72 = f32[256,16,128]{2,0,1:T(8,128)S(1)} all-to-all(f32[256,16,128]{2,0,1:T(8,128)S(1)} %copy_bitcast_fusion), channel_id=1, replica_groups=mesh['zh'=2,'y'=4,'x'=4,'zl'=4,'c'=2] {'y','x'}, dimensions={1} | all-to-all | bytes 4194304 | tf_op jit(solution)/shard_map/all_to_all | solution.py:73
  259.0 1.7 copy.59
  260.6 4.2 %all-to-all-start.5 = ((f32[256,2,64]{0,2,1:T(8,128)}), f32[256,2,64]{0,2,1:T(8,128)S(1)}, u32[]{:S(2)}, u32[]{:S(2)}) async-start(f32[256,2,64]{0,2,1:T(8,128)} %bitcast.21), calls=%async_computation.7 | async-start | bytes 262144 | tf_op jit(solution)/shard_map/all_to_all | solution.py:75
  264.8 2.7 copy_bitcast_fusion.1
  267.6 5.8 %all-to-all-done.5 = f32[256,2,64]{0,2,1:T(8,128)S(1)} async-done(((f32[256,2,64]{0,2,1:T(8,128)}), f32[256,2,64]{0,2,1:T(8,128)S(1)}, u32[]{:S(2)}, u32[]{:S(2)}) %all-to-all-start.5) | async-done | bytes 131104 | tf_op jit(solution)/shard_map/all_to_all | solution.py:75
  273.4 3.6 all-to-all-start
  277.0 0.9 constant_dynamic-slice_fusion.1
  278.5 0.8 constant_dynamic-slice_fusion.2
  279.4 9.8 %all-to-all-done = f32[96,16,128]{2,0,1:T(8,128)S(1)} async-done(((f32[96,16,128]{2,0,1:T(8,128)}), f32[96,16,128]{2,0,1:T(8,128)S(1)}, u32[]{:S(2)}, u32[]{:S(2)}) %all-to-all-start) | async-done | bytes 786464 | tf_op jit(solution)/shard_map/all_to_all | solution.py:73
  290.0 3.8 all-to-all-start.1
  293.8 8.0 %all-to-all-done.1 = f32[96,2,64]{0,2,1:T(8,128)S(1)} async-done(((f32[96,2,64]{0,2,1:T(8,128)}), f32[96,2,64]{0,2,1:T(8,128)S(1)}, u32[]{:S(2)}, u32[]{:S(2)}) %all-to-all-start.1) | async-done | bytes 49184 | tf_op jit(solution)/shard_map/all_to_all | solution.py:75
  302.5 3.4 all-to-all-start.6
  306.0 8.3 %all-to-all-done.6 = bf16[2,2,256,64]{2,3,1,0:T(8,128)(2,1)S(1)} async-done(((bf16[2,2,256,64]{2,3,1,0:T(8,128)(2,1)}), bf16[2,2,256,64]{2,3,1,0:T(8,128)(2,1)S(1)}, u32[]{:S(2)}, u32[]{:S(2)}) %all-to-all-start.6) | async-done | bytes 131104 | tf_op jit(solution)/shard_map/all_to_all | solution.py:82
  314.9 3.3 all-to-all-start.2
  318.3 7.9 %all-to-all-done.2 = bf16[2,2,96,64]{2,3,1,0:T(8,128)(2,1)S(1)} async-done(((bf16[2,2,96,64]{2,3,1,0:T(8,128)(2,1)}), bf16[2,2,96,64]{2,3,1,0:T(8,128)(2,1)S(1)}, u32[]{:S(2)}, u32[]{:S(2)}) %all-to-all-start.2) | async-done | bytes 49184 | tf_op jit(solution)/shard_map/all_to_all | solution.py:82
  326.2 1.8 broadcast_in_dim.55
  328.0 3.7 all-to-all-start.7
  331.9 25.1 %all-to-all-done.7 = bf16[16,2,256,128]{3,2,1,0:T(8,128)(2,1)S(1)} async-done(((bf16[16,2,256,128]{3,2,1,0:T(8,128)(2,1)}), bf16[16,2,256,128]{3,2,1,0:T(8,128)(2,1)S(1)}, u32[]{:S(2)}, u32[]{:S(2)}) %all-to-all-start.7) | async-done | bytes 2097184 | tf_op jit(solution)/shard_map/all_to_all | solution.py:84
  357.0 1.1 broadcast_in_dim.52
  358.0 4.3 %all-to-all-start.3 = ((bf16[16,2,96,128]{3,2,1,0:T(8,128)(2,1)}), bf16[16,2,96,128]{3,2,1,0:T(8,128)(2,1)}, u32[]{:S(2)}, u32[]{:S(2)}) async-start(bf16[16,2,96,128]{3,2,1,0:T(8,128)(2,1)} %broadcast_in_dim.52), calls=%async_computation.5 | async-start | bytes 1572864 | tf_op jit(solution)/shard_map/all_to_all | solution.py:84
  362.3 2.6 copy.63
  365.0 1.7 fusion.63
  366.7 1.4 copy.65
  368.1 1.4 copy.66
  369.5 4.4 %all-to-all-done.3 = bf16[16,2,96,128]{3,2,1,0:T(8,128)(2,1)} async-done(((bf16[16,2,96,128]{3,2,1,0:T(8,128)(2,1)}), bf16[16,2,96,128]{3,2,1,0:T(8,128)(2,1)}, u32[]{:S(2)}, u32[]{:S(2)}) %all-to-all-start.3) | async-done | bytes 786464 | tf_op jit(solution)/shard_map/all_to_all | solution.py:84
  373.9 1.2 fusion.64
  375.4 1.0 copy_bitcast_fusion.2
  (57 shorter events, 5.6 us)
Async XLA Ops:
  7.2 270.9 %copy-start = (bf16[256,2048]{1,0:T(8,128)(2,1)S(1)}, bf16[256,2048]{1,0:T(8,128)(2,1)}, u32[]{:S(2)}) copy-start(bf16[256,2048]{1,0:T(8,128)(2,1)} %param.21) | copy-start | bytes 3145732
  7.2 3.2 copy-start.9
  7.2 3.2 copy-start.1
  7.2 74.3 %all-gather.3.cloned.1.call-start = ((), (), s32[]{:S(2)}) async-start(), calls=%async_computation.12 | async-start | bytes 12255232 | tf_op jit(solution)/shard_map/all_gather | solution.py:102
  10.3 206.8 %reduce-scatter.3.cloned.1.call-start = ((), (), s32[]{:S(2)}) async-start(), calls=%async_computation.10 | async-start | bytes 9437184 | tf_op jit(solution)/shard_map/reduce_scatter | solution.py:132
  11.6 92.6 %copy-start.5 = (bf16[256,768]{1,0:T(8,128)(2,1)}, bf16[256,768]{1,0:T(8,128)(2,1)S(1)}, u32[]{:S(2)}) copy-start(bf16[256,768]{1,0:T(8,128)(2,1)S(1)} %gather_fusion) | copy-start | bytes 1179652
  105.2 6.8 %copy-start.2 = (f32[256,2048]{1,0:T(8,128)}, f32[256,2048]{1,0:T(8,128)S(1)}, u32[]{:S(2)}) copy-start(f32[256,2048]{1,0:T(8,128)S(1)} %convolution_multiply_fusion.1) | copy-start | bytes 6291460
  112.1 2.7 copy-start.10
  116.5 1.8 copy-start.3
  117.0 1.0 copy-start.7
  124.5 1.6 copy-start.4
  124.5 1.6 copy-start.6
  124.5 140.3 %reduce-scatter.5.cloned.1.call-start = ((), (), s32[]{:S(2)}) async-start(), calls=%async_computation.11 | async-start | bytes 3538944 | tf_op jit(solution)/shard_map/reduce_scatter | solution.py:150
  258.2 6.6 %copy-start.8 = (bf16[96,2048]{1,0:T(8,128)(2,1)S(1)}, bf16[96,2048]{1,0:T(8,128)(2,1)}, u32[]{:S(2)}) copy-start(bf16[96,2048]{1,0:T(8,128)(2,1)} %param.14) | copy-start | bytes 1179652
  260.6 12.8 %all-to-all-start.5 = ((f32[256,2,64]{0,2,1:T(8,128)}), f32[256,2,64]{0,2,1:T(8,128)S(1)}, u32[]{:S(2)}, u32[]{:S(2)}) async-start(f32[256,2,64]{0,2,1:T(8,128)} %bitcast.21), calls=%async_computation.7 | async-start | bytes 262144 | tf_op jit(solution)/shard_map/all_to_all | solution.py:75
  273.4 15.8 %all-to-all-start = ((f32[96,16,128]{2,0,1:T(8,128)}), f32[96,16,128]{2,0,1:T(8,128)S(1)}, u32[]{:S(2)}, u32[]{:S(2)}) async-start(f32[96,16,128]{2,0,1:T(8,128)} %copy_bitcast_fusion.1), calls=%async_computation.2 | async-start | bytes 1572864 | tf_op jit(solution)/shard_map/all_to_all | solution.py:73
  290.0 11.8 %all-to-all-start.1 = ((f32[96,2,64]{0,2,1:T(8,128)}), f32[96,2,64]{0,2,1:T(8,128)S(1)}, u32[]{:S(2)}, u32[]{:S(2)}) async-start(f32[96,2,64]{0,2,1:T(8,128)} %bitcast.13), calls=%async_computation.3 | async-start | bytes 131072 | tf_op jit(solution)/shard_map/all_to_all | solution.py:75
  302.5 11.8 %all-to-all-start.6 = ((bf16[2,2,256,64]{2,3,1,0:T(8,128)(2,1)}), bf16[2,2,256,64]{2,3,1,0:T(8,128)(2,1)S(1)}, u32[]{:S(2)}, u32[]{:S(2)}) async-start(bf16[2,2,256,64]{2,3,1,0:T(8,128)(2,1)} %broadcast_in_dim.53), calls=%async_computation.8 | async-start | bytes 262144 | tf_op jit(solution)/shard_map/all_to_all | solution.py:82
  314.9 11.3 %all-to-all-start.2 = ((bf16[2,2,96,64]{2,3,1,0:T(8,128)(2,1)}), bf16[2,2,96,64]{2,3,1,0:T(8,128)(2,1)S(1)}, u32[]{:S(2)}, u32[]{:S(2)}) async-start(bf16[2,2,96,64]{2,3,1,0:T(8,128)(2,1)} %broadcast_in_dim.50), calls=%async_computation.4 | async-start | bytes 131072 | tf_op jit(solution)/shard_map/all_to_all | solution.py:82
  328.0 29.0 %all-to-all-start.7 = ((bf16[16,2,256,128]{3,2,1,0:T(8,128)(2,1)}), bf16[16,2,256,128]{3,2,1,0:T(8,128)(2,1)S(1)}, u32[]{:S(2)}, u32[]{:S(2)}) async-start(bf16[16,2,256,128]{3,2,1,0:T(8,128)(2,1)} %broadcast_in_dim.55), calls=%async_computation.9 | async-start | bytes 4194304 | tf_op jit(solution)/shard_map/all_to_all | solution.py:84
  358.0 15.9 %all-to-all-start.3 = ((bf16[16,2,96,128]{3,2,1,0:T(8,128)(2,1)}), bf16[16,2,96,128]{3,2,1,0:T(8,128)(2,1)}, u32[]{:S(2)}, u32[]{:S(2)}) async-start(bf16[16,2,96,128]{3,2,1,0:T(8,128)(2,1)} %broadcast_in_dim.52), calls=%async_computation.5 | async-start | bytes 1572864 | tf_op jit(solution)/shard_map/all_to_all | solution.py:84
Sparse Core Ops, SparseCore 0:
  10.4 71.0 all-gather.2
  124.6 92.4 reduce-scatter.2
  219.7 43.1 reduce-scatter.4

commit v6 on v5

--- a/solution.py
+++ b/solution.py
@@ -100,10 +100,13 @@
         axis=0,
     )
     got = lax.all_gather(mine, ("zh",) + NARROW, axis=0, tiled=False)
-    got = got.reshape(halves, shards_n, r1 + r2, got.shape[-1]).transpose(1, 0, 2, 3)
-    first = got[:, :, :r1].reshape(shards_n * halves * r1, -1)
-    second = got[:, :, r1:].reshape(shards_n * halves * r2, -1)
-    return first, second
+    got = got.reshape(halves, shards_n, r1 + r2, got.shape[-1])
+    return got[:, :, :r1], got[:, :, r1:]
+
+
+def split_rows(x, like):
+    halves, shards_n, r = like.shape[:3]
+    return x.reshape(x.shape[0], shards_n, halves, r)
 
 
 def shards(
@@ -124,10 +127,18 @@
     scale_one = 1.0 / math.sqrt(PIX)
     scale_two = 1.0 / math.sqrt(MID)
     first_whole, second_whole = gather_weights(w_first, w_second)
-    hidden = jnp.dot(inputs, first_whole, preferred_element_type=jnp.float32) * scale_one
+    hidden = (
+        jnp.einsum("bnhr,hnrc->bc", split_rows(inputs, first_whole), first_whole,
+                   preferred_element_type=jnp.float32)
+        * scale_one
+    )
     active_full, gelu_back = jax.vjp(jax.nn.gelu, hidden)
     active = active_full.astype(jnp.bfloat16)
-    embedded = jnp.dot(active, second_whole, preferred_element_type=jnp.float32) * scale_two
+    embedded = (
+        jnp.einsum("bnhr,hnrc->bc", split_rows(active, second_whole), second_whole,
+                   preferred_element_type=jnp.float32)
+        * scale_two
+    )
     embed_half = embed_gradient(embedded, partner)
     grad_second = lax.psum_scatter(
         (scale_two * jnp.dot(active.T, embed_half, preferred_element_type=jnp.float32)).astype(
@@ -137,9 +148,9 @@
         scatter_dimension=0,
         tiled=True,
     ).astype(jnp.float32)
-    active_grad = scale_two * jnp.dot(
-        embed_half, second_whole.T, preferred_element_type=jnp.float32
-    )
+    active_grad = scale_two * jnp.einsum(
+        "bc,hnrc->bnhr", embed_half, second_whole, preferred_element_type=jnp.float32
+    ).reshape(active.shape)
     hidden_half = gelu_back(active_grad)[0].astype(jnp.bfloat16)
     term_first = (
         scale_one * jnp.dot(inputs.T, hidden_half, preferred_element_type=jnp.float32)

time: 387 us -> 368 us (0.951)
  local copies, waits for them, and re-layouts: 48.4 us -> 33.7 us
  waiting for transfers between devices: 221 us -> 212 us
  matrix products: 26.6 us -> 31.9 us
    slice x4 -> x0, local copies, waits for them, and re-layouts: 22.7 us -> none  [the longest x2 16.6 us: gather_weights(): second = got[:, :, r1:].reshape(shards_n * halves * r2, -1)]
    dot_general x2 -> x3, matrix products: 7.89 us -> 17.2 us  [the longest x1 7.13 us: shards(): jnp.einsum('bc,hnrc->bnhr', embed_half, second_whole, preferred_element_t...]
    reduce_scatter x1, waiting for transfers between devices: 81.5 us -> 72.3 us  [shards(): lax.psum_scatter((scale_two * jnp.dot(active.T, embed_half, preferred_ele...]
    mul x0 -> x2, local copies, waits for them, and re-layouts: none -> 5.9 us  [shards(): scale_two * jnp.einsum('bc,hnrc->bnhr', embed_half, second_whole, preferr...]
  transfers between devices with their start and end apart: 10 -> 10, of which waited for: 9 -> 9; matrix products, arithmetic and copies ran while one was open for 8% -> 11% of each run, Pallas kernels for 0% -> 0%
where the time goes in v6:
time: 368 us; the launch traced here: 364 us
  waiting for transfers between devices  212 us (58%)
  blocking collectives  36.2 us (10%)
  local copies, waits for them, and re-layouts  33.7 us (9%)
  matrix products  31.9 us (9%)
  starting transfers between devices  26.5 us (7%)
  between operations  14.1 us (4%)
  other arithmetic  10.3 us (3%)
    reduce_scatter x1, waiting for transfers between devices, shards(): lax.psum_scatter((scale_two * jnp.dot(active.T, embed_half, preferred_ele...  72.3 us
    all_gather x1, waiting for transfers between devices, gather_weights(): got = lax.all_gather(mine, ('zh',) + NARROW, axis=0, tiled=False)  69.7 us
    all_to_all x1, blocking collectives, wide_mean_update(): got = lax.all_to_all(delta, plane, 1, 0, tiled=True)  36.2 us
    all_to_all x2, waiting for transfers between devices, wide_mean_update(): lax.all_to_all(jnp.broadcast_to(back[None], (n_plane,) + back.shape), pla...  29.6 us
    all_to_all x2, waiting for transfers between devices, wide_mean_update(): lax.all_to_all(jnp.broadcast_to(both[None], (n_half,) + both.shape), 'zh'...  16.2 us
    all_to_all x2, waiting for transfers between devices, wide_mean_update(): got = lax.all_to_all(part, 'zh', 1, 0, tiled=True)  13.8 us
    all_to_all x1, waiting for transfers between devices, wide_mean_update(): got = lax.all_to_all(delta, plane, 1, 0, tiled=True)  9.85 us
    all_to_all x2, starting transfers between devices, wide_mean_update(): lax.all_to_all(jnp.broadcast_to(back[None], (n_plane,) + back.shape), pla...  8 us
  transfers between devices with their start and end apart: 10, of which 9 were waited for; matrix products, arithmetic and copies ran while one was open for 11% of the time, Pallas kernels for 0%

profile of v6, /device:TPU:64, one launch (start us, length us, event | category | flops | bytes accessed | tf_op | source)
XLA Modules:
  0.0 364.2 jit_solution(12933542262264659554)
XLA Ops:
  7.3 1.2 constant_dynamic-slice_fusion.3
  8.4 0.9 constant_dynamic-slice_fusion.4
  9.4 0.9 pad_maximum_fusion
  10.4 1.2 gather_fusion
  11.8 69.7 %all-gather.3.cloned.1.call-done = bf16[2816,2048]{1,0:T(8,128)(2,1)} async-done(((bf16[176,2048]{1,0:T(8,128)(2,1)}), bf16[2816,2048]{1,0:T(8,128)(2,1)}) %all-gather.3.cloned.1.call-update) | async-done | bytes 11534352 | tf_op jit(solution)/shard_map/all_gather | solution.py:102
  81.5 4.8 %multiply_convert_fusion.3 = (bf16[256,2048]{1,0:T(8,128)(2,1)S(1)}, f32[256,2048]{1,0:T(8,128)}) fusion(bf16[2,8,176,2048]{3,2,1,0:T(8,128)(2,1)} %bitcast.111, bf16[256,8,2,48]{0,3,2,1:T(8,128)(2,1)S(1)} %bitcast.106, pred[256]{0:T(512)(128)(4,1)S(1)} %compare_and_fusion), kind=kOutput, calls=%fused_computation.35 | convolution fusion | flops 810745856 | bytes 6684928 | tf_op jit(solution)/shard_map/bnhr,hnrc->bc/dot_general | solution.py:131
  86.3 1.0 copy-done.4
  87.3 1.5 reshape.114
  88.8 5.2 %multiply_reduce_fusion.1 = (f32[256]{0:T(256)S(1)}, f32[256,2048]{1,0:T(8,128)S(1)}) fusion(bf16[2,8,176,2048]{3,2,1,0:T(8,128)(2,1)} %bitcast.112, bf16[256,8,2,128]{3,2,1,0:T(2,128)(2,1)} %reshape.114), kind=kOutput, calls=%fused_computation.34 | convolution fusion | flops 2149056256 | bytes 11535360 | tf_op jit(solution)/shard_map/bnhr,hnrc->bc/dot_general | solution.py:138
  94.1 1.3 convolution_multiply_fusion.1
  95.4 1.1 copy.51
  96.8 1.7 multiply_reduce_fusion
  99.0 1.0 copy-done.6
  100.0 5.7 %multiply_convert_fusion = bf16[2048,2048]{1,0:T(8,128)(2,1)} fusion(bf16[256,2048]{1,0:T(8,128)(2,1)S(1)} %copy-done.5, bf16[256,2048]{1,0:T(8,128)(2,1)S(1)} %multiply_convert_fusion.2), kind=kOutput, calls=%fused_computation.1 | convolution fusion | flops 2155872256 | bytes 10485760 | tf_op jit(solution)/shard_map/dot_general | solution.py:144
  105.9 1.0 copy-done.7
  106.9 7.1 %multiply_bitcast_fusion = f32[256,8,2,128]{0,3,1,2:T(8,128)} fusion(bf16[2,8,176,2048]{3,2,1,0:T(8,128)(2,1)} %bitcast.113, bf16[256,2048]{1,0:T(8,128)(2,1)S(1)} %copy-done.7), kind=kOutput, calls=%fused_computation.31 | convolution fusion | flops 2148007936 | bytes 11534336 | tf_op jit(solution)/shard_map/bc,hnrc->bnhr/dot_general | solution.py:151
  114.0 3.2 copy.52
  117.3 2.7 mul.276
  119.9 6.1 %multiply_convert_fusion.1 = bf16[768,2048]{1,0:T(8,128)(2,1)} fusion(f32[256,2048]{1,0:T(8,128)} %get-tuple-element.23, f32[256,2048]{1,0:T(8,128)} %mul.276, bf16[256,768]{1,0:T(8,128)(2,1)S(1)} %copy-done.3, pred[256]{0:T(512)(128)(4,1)S(1)} %compare_and_fusion), kind=kOutput, calls=%fused_computation.6 | convolution fusion | flops 819134464 | bytes 7733504 | tf_op jit(solution)/shard_map/dot_general | solution.py:156
  126.0 72.3 %reduce-scatter.3.cloned.1.call-done = bf16[256,2048]{1,0:T(8,128)(2,1)} async-done(((bf16[2048,2048]{1,0:T(8,128)(2,1)}), bf16[256,2048]{1,0:T(8,128)(2,1)}) %reduce-scatter.3.cloned.1.call-update) | async-done | bytes 1048592 | tf_op jit(solution)/shard_map/reduce_scatter | solution.py:143
  198.3 1.5 convert_element_type.90
  199.8 3.4 copy_bitcast_fusion
  203.2 36.2 %all_to_all.72 = f32[256,16,128]{2,0,1:T(8,128)S(1)} all-to-all(f32[256,16,128]{2,0,1:T(8,128)S(1)} %copy_bitcast_fusion), channel_id=1, replica_groups=mesh['zh'=2,'y'=4,'x'=4,'zl'=4,'c'=2] {'y','x'}, dimensions={1} | all-to-all | bytes 4194304 | tf_op jit(solution)/shard_map/all_to_all | solution.py:73
  240.2 1.7 copy.63
  241.8 4.2 %all-to-all-start.5 = ((f32[256,2,64]{0,2,1:T(8,128)}), f32[256,2,64]{0,2,1:T(8,128)S(1)}, u32[]{:S(2)}, u32[]{:S(2)}) async-start(f32[256,2,64]{0,2,1:T(8,128)} %bitcast.26), calls=%async_computation.7 | async-start | bytes 262144 | tf_op jit(solution)/shard_map/all_to_all | solution.py:75
  246.0 2.7 copy_bitcast_fusion.1
  248.8 5.8 %all-to-all-done.5 = f32[256,2,64]{0,2,1:T(8,128)S(1)} async-done(((f32[256,2,64]{0,2,1:T(8,128)}), f32[256,2,64]{0,2,1:T(8,128)S(1)}, u32[]{:S(2)}, u32[]{:S(2)}) %all-to-all-start.5) | async-done | bytes 131104 | tf_op jit(solution)/shard_map/all_to_all | solution.py:75
  254.6 3.6 all-to-all-start
  259.5 0.9 constant_dynamic-slice_fusion.1
  260.6 9.9 %all-to-all-done = f32[96,16,128]{2,0,1:T(8,128)S(1)} async-done(((f32[96,16,128]{2,0,1:T(8,128)}), f32[96,16,128]{2,0,1:T(8,128)S(1)}, u32[]{:S(2)}, u32[]{:S(2)}) %all-to-all-start) | async-done | bytes 786464 | tf_op jit(solution)/shard_map/all_to_all | solution.py:73
  271.3 3.7 %all-to-all-start.1 = ((f32[96,2,64]{0,2,1:T(8,128)}), f32[96,2,64]{0,2,1:T(8,128)S(1)}, u32[]{:S(2)}, u32[]{:S(2)}) async-start(f32[96,2,64]{0,2,1:T(8,128)} %bitcast.18), calls=%async_computation.3 | async-start | bytes 131072 | tf_op jit(solution)/shard_map/all_to_all | solution.py:75
  275.0 8.0 %all-to-all-done.1 = f32[96,2,64]{0,2,1:T(8,128)S(1)} async-done(((f32[96,2,64]{0,2,1:T(8,128)}), f32[96,2,64]{0,2,1:T(8,128)S(1)}, u32[]{:S(2)}, u32[]{:S(2)}) %all-to-all-start.1) | async-done | bytes 49184 | tf_op jit(solution)/shard_map/all_to_all | solution.py:75
  283.7 3.4 all-to-all-start.6
  287.1 8.3 %all-to-all-done.6 = bf16[2,2,256,64]{2,3,1,0:T(8,128)(2,1)S(1)} async-done(((bf16[2,2,256,64]{2,3,1,0:T(8,128)(2,1)}), bf16[2,2,256,64]{2,3,1,0:T(8,128)(2,1)S(1)}, u32[]{:S(2)}, u32[]{:S(2)}) %all-to-all-start.6) | async-done | bytes 131104 | tf_op jit(solution)/shard_map/all_to_all | solution.py:82
  296.1 3.3 all-to-all-start.2
  299.5 7.9 %all-to-all-done.2 = bf16[2,2,96,64]{2,3,1,0:T(8,128)(2,1)S(1)} async-done(((bf16[2,2,96,64]{2,3,1,0:T(8,128)(2,1)}), bf16[2,2,96,64]{2,3,1,0:T(8,128)(2,1)S(1)}, u32[]{:S(2)}, u32[]{:S(2)}) %all-to-all-start.2) | async-done | bytes 49184 | tf_op jit(solution)/shard_map/all_to_all | solution.py:82
  307.4 1.8 broadcast_in_dim.61
  309.2 3.7 %all-to-all-start.7 = ((bf16[16,2,256,128]{3,2,1,0:T(8,128)(2,1)}), bf16[16,2,256,128]{3,2,1,0:T(8,128)(2,1)S(1)}, u32[]{:S(2)}, u32[]{:S(2)}) async-start(bf16[16,2,256,128]{3,2,1,0:T(8,128)(2,1)} %broadcast_in_dim.61), calls=%async_computation.9 | async-start | bytes 4194304 | tf_op jit(solution)/shard_map/all_to_all | solution.py:84
  313.1 25.1 %all-to-all-done.7 = bf16[16,2,256,128]{3,2,1,0:T(8,128)(2,1)S(1)} async-done(((bf16[16,2,256,128]{3,2,1,0:T(8,128)(2,1)}), bf16[16,2,256,128]{3,2,1,0:T(8,128)(2,1)S(1)}, u32[]{:S(2)}, u32[]{:S(2)}) %all-to-all-start.7) | async-done | bytes 2097184 | tf_op jit(solution)/shard_map/all_to_all | solution.py:84
  338.2 1.0 broadcast_in_dim.58
  339.2 4.3 %all-to-all-start.3 = ((bf16[16,2,96,128]{3,2,1,0:T(8,128)(2,1)}), bf16[16,2,96,128]{3,2,1,0:T(8,128)(2,1)}, u32[]{:S(2)}, u32[]{:S(2)}) async-start(bf16[16,2,96,128]{3,2,1,0:T(8,128)(2,1)} %broadcast_in_dim.58), calls=%async_computation.5 | async-start | bytes 1572864 | tf_op jit(solution)/shard_map/all_to_all | solution.py:84
  343.5 2.6 copy.67
  346.1 1.7 fusion.77
  347.8 1.4 copy.69
  349.2 1.4 copy.70
  350.7 4.5 %all-to-all-done.3 = bf16[16,2,96,128]{3,2,1,0:T(8,128)(2,1)} async-done(((bf16[16,2,96,128]{3,2,1,0:T(8,128)(2,1)}), bf16[16,2,96,128]{3,2,1,0:T(8,128)(2,1)}, u32[]{:S(2)}, u32[]{:S(2)}) %all-to-all-start.3) | async-done | bytes 786464 | tf_op jit(solution)/shard_map/all_to_all | solution.py:84
  355.1 1.2 fusion.78
  356.6 1.0 copy_bitcast_fusion.2
  (58 shorter events, 6.3 us)
Async XLA Ops:
  7.2 252.2 %copy-start = (bf16[256,2048]{1,0:T(8,128)(2,1)S(1)}, bf16[256,2048]{1,0:T(8,128)(2,1)}, u32[]{:S(2)}) copy-start(bf16[256,2048]{1,0:T(8,128)(2,1)} %param.21) | copy-start | bytes 3145732
  7.2 3.2 copy-start.9
  7.2 3.2 copy-start.1
  7.2 74.3 %all-gather.3.cloned.1.call-start = ((), (), s32[]{:S(2)}) async-start(), calls=%async_computation.12 | async-start | bytes 12255232 | tf_op jit(solution)/shard_map/all_gather | solution.py:102
  10.3 188.0 %reduce-scatter.3.cloned.1.call-start = ((), (), s32[]{:S(2)}) async-start(), calls=%async_computation.10 | async-start | bytes 9437184 | tf_op jit(solution)/shard_map/reduce_scatter | solution.py:143
  11.6 74.8 %copy-start.2 = (bf16[256,768]{1,0:T(8,128)(2,1)}, bf16[256,768]{1,0:T(8,128)(2,1)S(1)}, u32[]{:S(2)}) copy-start(bf16[256,768]{1,0:T(8,128)(2,1)S(1)} %gather_fusion) | copy-start | bytes 1179652
  86.3 1.0 copy-start.4
  94.1 2.7 copy-start.10
  98.5 1.5 copy-start.5
  99.0 1.0 copy-start.6
  105.7 1.2 copy-start.7
  105.7 140.3 %reduce-scatter.5.cloned.1.call-start = ((), (), s32[]{:S(2)}) async-start(), calls=%async_computation.11 | async-start | bytes 3538944 | tf_op jit(solution)/shard_map/reduce_scatter | solution.py:161
  117.2 2.7 copy-start.3
  239.4 6.6 %copy-start.8 = (bf16[96,2048]{1,0:T(8,128)(2,1)S(1)}, bf16[96,2048]{1,0:T(8,128)(2,1)}, u32[]{:S(2)}) copy-start(bf16[96,2048]{1,0:T(8,128)(2,1)} %param.14) | copy-start | bytes 1179652
  241.8 12.7 %all-to-all-start.5 = ((f32[256,2,64]{0,2,1:T(8,128)}), f32[256,2,64]{0,2,1:T(8,128)S(1)}, u32[]{:S(2)}, u32[]{:S(2)}) async-start(f32[256,2,64]{0,2,1:T(8,128)} %bitcast.26), calls=%async_computation.7 | async-start | bytes 262144 | tf_op jit(solution)/shard_map/all_to_all | solution.py:75
  254.6 15.9 %all-to-all-start = ((f32[96,16,128]{2,0,1:T(8,128)}), f32[96,16,128]{2,0,1:T(8,128)S(1)}, u32[]{:S(2)}, u32[]{:S(2)}) async-start(f32[96,16,128]{2,0,1:T(8,128)} %copy_bitcast_fusion.1), calls=%async_computation.2 | async-start | bytes 1572864 | tf_op jit(solution)/shard_map/all_to_all | solution.py:73
  271.3 11.8 %all-to-all-start.1 = ((f32[96,2,64]{0,2,1:T(8,128)}), f32[96,2,64]{0,2,1:T(8,128)S(1)}, u32[]{:S(2)}, u32[]{:S(2)}) async-start(f32[96,2,64]{0,2,1:T(8,128)} %bitcast.18), calls=%async_computation.3 | async-start | bytes 131072 | tf_op jit(solution)/shard_map/all_to_all | solution.py:75
  283.7 11.8 %all-to-all-start.6 = ((bf16[2,2,256,64]{2,3,1,0:T(8,128)(2,1)}), bf16[2,2,256,64]{2,3,1,0:T(8,128)(2,1)S(1)}, u32[]{:S(2)}, u32[]{:S(2)}) async-start(bf16[2,2,256,64]{2,3,1,0:T(8,128)(2,1)} %broadcast_in_dim.59), calls=%async_computation.8 | async-start | bytes 262144 | tf_op jit(solution)/shard_map/all_to_all | solution.py:82
  296.1 11.3 %all-to-all-start.2 = ((bf16[2,2,96,64]{2,3,1,0:T(8,128)(2,1)}), bf16[2,2,96,64]{2,3,1,0:T(8,128)(2,1)S(1)}, u32[]{:S(2)}, u32[]{:S(2)}) async-start(bf16[2,2,96,64]{2,3,1,0:T(8,128)(2,1)} %broadcast_in_dim.56), calls=%async_computation.4 | async-start | bytes 131072 | tf_op jit(solution)/shard_map/all_to_all | solution.py:82
  309.2 29.0 %all-to-all-start.7 = ((bf16[16,2,256,128]{3,2,1,0:T(8,128)(2,1)}), bf16[16,2,256,128]{3,2,1,0:T(8,128)(2,1)S(1)}, u32[]{:S(2)}, u32[]{:S(2)}) async-start(bf16[16,2,256,128]{3,2,1,0:T(8,128)(2,1)} %broadcast_in_dim.61), calls=%async_computation.9 | async-start | bytes 4194304 | tf_op jit(solution)/shard_map/all_to_all | solution.py:84
  339.2 15.9 %all-to-all-start.3 = ((bf16[16,2,96,128]{3,2,1,0:T(8,128)(2,1)}), bf16[16,2,96,128]{3,2,1,0:T(8,128)(2,1)}, u32[]{:S(2)}, u32[]{:S(2)}) async-start(bf16[16,2,96,128]{3,2,1,0:T(8,128)(2,1)} %broadcast_in_dim.58), calls=%async_computation.5 | async-start | bytes 1572864 | tf_op jit(solution)/shard_map/all_to_all | solution.py:84
Sparse Core Ops, SparseCore 0:
  10.4 71.0 all-gather.2
  105.8 92.4 reduce-scatter.2
  200.9 43.1 reduce-scatter.4

commit v7 on v6

--- a/solution.py
+++ b/solution.py
@@ -62,7 +62,15 @@
     return embed_grad.astype(jnp.bfloat16)
 
 
-def wide_mean_update(delta, momentum, weights):
+def plane_sum(delta):
+    plane = ("y", "x")
+    n_plane = lax.axis_size(plane)
+    rows, cols = delta.shape
+    got = lax.all_to_all(delta, plane, 1, 0, tiled=True)
+    return jnp.sum(got.reshape(n_plane, rows, cols // n_plane), axis=0)
+
+
+def wide_mean_update(delta, momentum, weights, part=None):
     plane = ("y", "x")
     n_plane = lax.axis_size(plane)
     n_half = lax.axis_size("zh")
@@ -70,8 +78,7 @@
     rows, cols = delta.shape
     p1 = cols // n_plane
     p2 = p1 // n_half
-    got = lax.all_to_all(delta, plane, 1, 0, tiled=True)
-    part = jnp.sum(got.reshape(n_plane, rows, p1), axis=0)
+    part = plane_sum(delta) if part is None else part
     got = lax.all_to_all(part, "zh", 1, 0, tiled=True)
     mean = jnp.sum(got.reshape(n_half, rows, p2), axis=0) / sites
     start = lax.axis_index(plane) * p1 + lax.axis_index("zh") * p2
@@ -140,14 +147,12 @@
         * scale_two
     )
     embed_half = embed_gradient(embedded, partner)
-    grad_second = lax.psum_scatter(
-        (scale_two * jnp.dot(active.T, embed_half, preferred_element_type=jnp.float32)).astype(
-            jnp.bfloat16
-        ),
-        NARROW,
-        scatter_dimension=0,
-        tiled=True,
-    ).astype(jnp.float32)
+    term_second = (
+        scale_two * jnp.dot(active.T, embed_half, preferred_element_type=jnp.float32)
+    ).astype(jnp.bfloat16)
+    cols = term_second.shape[1] // 2
+    first_part, second_part = term_second[:, :cols], term_second[:, cols:]
+    grad_a = lax.psum_scatter(first_part, NARROW, scatter_dimension=0, tiled=True)
     active_grad = scale_two * jnp.einsum(
         "bc,hnrc->bnhr", embed_half, second_whole, preferred_element_type=jnp.float32
     ).reshape(active.shape)
@@ -155,9 +160,22 @@
     term_first = (
         scale_one * jnp.dot(inputs.T, hidden_half, preferred_element_type=jnp.float32)
     ).astype(jnp.bfloat16)
-    term_first, grad_second = lax.optimization_barrier((term_first, grad_second))
-    delta_second = adam_delta(grad_second, m_second[0], v_second[0], w_second)
-    new_second, vel_second = wide_mean_update(delta_second, mom_second, w_second)
+    left = slice(0, cols)
+    right = slice(cols, 2 * cols)
+    delta_a = adam_delta(
+        grad_a.astype(jnp.float32), m_second[0][:, left], v_second[0][:, left], w_second[:, left]
+    )
+    plane_a = plane_sum(delta_a)
+    second_part, plane_a = lax.optimization_barrier((second_part, plane_a))
+    grad_b = lax.psum_scatter(second_part, NARROW, scatter_dimension=0, tiled=True)
+    out_a = wide_mean_update(delta_a, mom_second[:, left], w_second[:, left], plane_a)
+    term_first, grad_b = lax.optimization_barrier((term_first, grad_b))
+    delta_b = adam_delta(
+        grad_b.astype(jnp.float32), m_second[0][:, right], v_second[0][:, right], w_second[:, right]
+    )
+    out_b = wide_mean_update(delta_b, mom_second[:, right], w_second[:, right])
+    new_second = jnp.concatenate([out_a[0], out_b[0]], axis=1)
+    vel_second = jnp.concatenate([out_a[1], out_b[1]], axis=1)
     grad_first = lax.psum_scatter(
         term_first, NARROW, scatter_dimension=0, tiled=True
     ).astype(jnp.float32)

time: 368 us -> 415 us (1.13)
  waiting for transfers between devices: 212 us -> 243 us
  starting transfers between devices: 26.5 us -> 43.8 us
  blocking collectives: 36.2 us -> 24.5 us
  local copies, waits for them, and re-layouts: 33.7 us -> 39.6 us
  other arithmetic: 10.3 us -> 15.7 us
  matrix products: 31.9 us -> 26.8 us
    all_to_all x1 -> x2, waiting for transfers between devices: 9.85 us -> 24.9 us  [plane_sum(): got = lax.all_to_all(delta, plane, 1, 0, tiled=True)]
    all_to_all x1, blocking collectives: 36.2 us -> 24.5 us  [plane_sum(): got = lax.all_to_all(delta, plane, 1, 0, tiled=True)]
    slice x0 -> x3, local copies, waits for them, and re-layouts: none -> 7.16 us  [the longest x1 3.92 us: shards(): first_part, second_part = (term_second[:, :cols], term_second[:, cols:])]
    all_to_all x1 -> x2, starting transfers between devices: 3.61 us -> 10.4 us  [plane_sum(): got = lax.all_to_all(delta, plane, 1, 0, tiled=True)]
    all_to_all x2 -> x3, waiting for transfers between devices: 13.8 us -> 19.9 us  [wide_mean_update(): got = lax.all_to_all(part, 'zh', 1, 0, tiled=True)]
    reduce_scatter x1 -> x2, waiting for transfers between devices: 72.3 us -> 77.4 us  [the longest x1 48 us: shards(): lax.psum_scatter(first_part, NARROW, scatter_dimension=0, tiled=True)]
    unnamed x28 -> x52, local copies, waits for them, and re-layouts: 6.15 us -> 10.9 us
    mul x0 -> x2, other arithmetic: none -> 4.7 us  [adam_delta(): rate_inner * (moment_one / (jnp.sqrt(moment_two) + adam_eps) + weight_dec...]
  transfers between devices with their start and end apart: 10 -> 15, of which waited for: 9 -> 14; matrix products, arithmetic and copies ran while one was open for 11% -> 12% of each run, Pallas kernels for 0% -> 0%
where the time goes in v7:
time: 415 us; the launch traced here: 408 us
  waiting for transfers between devices  243 us (59%)
  starting transfers between devices  43.8 us (11%)
  local copies, waits for them, and re-layouts  39.6 us (10%)
  matrix products  26.8 us (6%)
  blocking collectives  24.5 us (6%)
  other arithmetic  15.7 us (4%)
  between operations  14.3 us (3%)
    all_gather x1, waiting for transfers between devices, gather_weights(): got = lax.all_gather(mine, ('zh',) + NARROW, axis=0, tiled=False)  69.7 us
    reduce_scatter x1, waiting for transfers between devices, shards(): lax.psum_scatter(first_part, NARROW, scatter_dimension=0, tiled=True)  48 us
    all_to_all x3, waiting for transfers between devices, wide_mean_update(): lax.all_to_all(jnp.broadcast_to(back[None], (n_plane,) + back.shape), pla...  30.7 us
    reduce_scatter x1, waiting for transfers between devices, shards(): lax.psum_scatter(second_part, NARROW, scatter_dimension=0, tiled=True)  29.5 us
    all_to_all x2, waiting for transfers between devices, plane_sum(): got = lax.all_to_all(delta, plane, 1, 0, tiled=True)  24.9 us
    all_to_all x1, blocking collectives, plane_sum(): got = lax.all_to_all(delta, plane, 1, 0, tiled=True)  24.5 us
    all_to_all x3, waiting for transfers between devices, wide_mean_update(): lax.all_to_all(jnp.broadcast_to(both[None], (n_half,) + both.shape), 'zh'...  20.4 us
    all_to_all x3, waiting for transfers between devices, wide_mean_update(): got = lax.all_to_all(part, 'zh', 1, 0, tiled=True)  19.9 us
  transfers between devices with their start and end apart: 15, of which 14 were waited for; matrix products, arithmetic and copies ran while one was open for 12% of the time, Pallas kernels for 0%

profile of v7, /device:TPU:64, one launch (start us, length us, event | category | flops | bytes accessed | tf_op | source)
XLA Modules:
  0.0 408.0 jit_solution(14671550227496455031)
XLA Ops:
  7.3 1.2 constant_dynamic-slice_fusion.3
  10.4 1.2 gather_fusion
  11.8 69.7 %all-gather.3.cloned.1.call-done = bf16[2816,2048]{1,0:T(8,128)(2,1)} async-done(((bf16[176,2048]{1,0:T(8,128)(2,1)}), bf16[2816,2048]{1,0:T(8,128)(2,1)}) %all-gather.3.cloned.1.call-update) | async-done | bytes 11534352 | tf_op jit(solution)/shard_map/all_gather | solution.py:109
  81.5 4.8 %multiply_convert_fusion.3 = (bf16[256,2048]{1,0:T(8,128)(2,1)S(1)}, f32[256,2048]{1,0:T(8,128)}) fusion(bf16[2,8,176,2048]{3,2,1,0:T(8,128)(2,1)} %bitcast.124, bf16[256,8,2,48]{0,3,2,1:T(8,128)(2,1)S(1)} %bitcast.116, pred[256]{0:T(512)(128)(4,1)S(1)} %compare_and_fusion), kind=kOutput, calls=%fused_computation.26 | convolution fusion | flops 810745856 | bytes 6684928 | tf_op jit(solution)/shard_map/bnhr,hnrc->bc/dot_general | solution.py:138
  88.1 5.0 %multiply_reduce_fusion.1 = (f32[256]{0:T(256)S(1)}, f32[256,2048]{1,0:T(8,128)S(1)}) fusion(bf16[2,8,176,2048]{3,2,1,0:T(8,128)(2,1)} %bitcast.125, bf16[256,8,2,128]{3,2,1,0:T(2,128)(2,1)S(1)} %reshape.125), kind=kOutput, calls=%fused_computation.25 | convolution fusion | flops 2149056256 | bytes 11535360 | tf_op jit(solution)/shard_map/bnhr,hnrc->bc/dot_general | solution.py:145
  96.1 2.4 multiply_convert_fusion
  98.5 3.9 fusion.87
  102.5 1.1 copy-done.4
  105.3 1.5 copy.93
  106.8 48.0 %reduce-scatter.4.cloned.1.call-done = bf16[256,1024]{0,1:T(8,128)(2,1)} async-done(((bf16[2048,1024]{0,1:T(8,128)(2,1)}), bf16[256,1024]{0,1:T(8,128)(2,1)}) %reduce-scatter.4.cloned.1.call-update) | async-done | bytes 524304 | tf_op jit(solution)/shard_map/reduce_scatter | solution.py:155
  154.8 1.9 fusion.27
  156.6 24.5 %all_to_all.108 = f32[256,16,64]{0,2,1:T(8,128)S(1)} all-to-all(f32[256,16,64]{0,2,1:T(8,128)S(1)} %bitcast.102), channel_id=1, replica_groups=mesh['zh'=2,'y'=4,'x'=4,'zl'=4,'c'=2] {'y','x'}, dimensions={1} | all-to-all | bytes 2097152 | tf_op jit(solution)/shard_map/all_to_all | solution.py:69
  183.1 7.1 %multiply_bitcast_fusion = f32[256,8,2,128]{0,3,1,2:T(8,128)} fusion(bf16[2,8,176,2048]{3,2,1,0:T(8,128)(2,1)} %bitcast.126, bf16[256,2048]{1,0:T(8,128)(2,1)S(1)} %copy-done.15), kind=kOutput, calls=%fused_computation.22 | convolution fusion | flops 2148007936 | bytes 11534336 | tf_op jit(solution)/shard_map/bc,hnrc->bnhr/dot_general | solution.py:156
  190.2 3.2 copy.91
  193.4 2.7 mul.292
  196.1 6.2 %multiply_convert_fusion.1 = bf16[768,2048]{1,0:T(8,128)(2,1)} fusion(f32[256,2048]{1,0:T(8,128)} %get-tuple-element.49, f32[256,2048]{1,0:T(8,128)} %mul.292, bf16[256,768]{1,0:T(8,128)(2,1)} %copy-done.10, pred[256]{0:T(512)(128)(4,1)S(1)} %compare_and_fusion), kind=kOutput, calls=%fused_computation.6 | convolution fusion | flops 819134464 | bytes 7733504 | tf_op jit(solution)/shard_map/dot_general | solution.py:161
  202.3 29.5 %reduce-scatter.6.cloned.1.call-done = bf16[256,1024]{0,1:T(8,128)(2,1)} async-done(((bf16[2048,1024]{0,1:T(8,128)(2,1)}), bf16[256,1024]{0,1:T(8,128)(2,1)}) %reduce-scatter.6.cloned.1.call-update) | async-done | bytes 524304 | tf_op jit(solution)/shard_map/reduce_scatter | solution.py:170
  232.1 2.3 fusion.90
  234.4 5.6 %all-to-all-start.5 = ((f32[256,2,32]{0,2,1:T(8,128)}), f32[256,2,32]{0,2,1:T(8,128)}, u32[]{:S(2)}, u32[]{:S(2)}) async-start(f32[256,2,32]{0,2,1:T(8,128)} %bitcast.117), calls=%async_computation.8 | async-start | bytes 131072 | tf_op jit(solution)/shard_map/all_to_all | solution.py:82
  241.7 6.5 %all-to-all-done.5 = f32[256,2,32]{0,2,1:T(8,128)} async-done(((f32[256,2,32]{0,2,1:T(8,128)}), f32[256,2,32]{0,2,1:T(8,128)}, u32[]{:S(2)}, u32[]{:S(2)}) %all-to-all-start.5) | async-done | bytes 65568 | tf_op jit(solution)/shard_map/all_to_all | solution.py:82
  250.4 3.3 all-to-all-start.6
  253.8 2.8 fusion.31
  256.6 6.3 %all-to-all-done.6 = bf16[2,2,256,32]{2,3,1,0:T(8,128)(2,1)S(1)} async-done(((bf16[2,2,256,32]{2,3,1,0:T(8,128)(2,1)}), bf16[2,2,256,32]{2,3,1,0:T(8,128)(2,1)S(1)}, u32[]{:S(2)}, u32[]{:S(2)}) %all-to-all-start.6) | async-done | bytes 65568 | tf_op jit(solution)/shard_map/all_to_all | solution.py:89
  262.9 6.8 %all-to-all-start.8 = ((f32[256,16,64]{0,2,1:T(8,128)}), f32[256,16,64]{0,2,1:T(8,128)S(1)}, u32[]{:S(2)}, u32[]{:S(2)}) async-start(f32[256,16,64]{0,2,1:T(8,128)} %bitcast.34), calls=%async_computation.11 | async-start | bytes 2097152 | tf_op jit(solution)/shard_map/all_to_all | solution.py:69
  269.8 15.1 %all-to-all-done.8 = f32[256,16,64]{0,2,1:T(8,128)S(1)} async-done(((f32[256,16,64]{0,2,1:T(8,128)}), f32[256,16,64]{0,2,1:T(8,128)S(1)}, u32[]{:S(2)}, u32[]{:S(2)}) %all-to-all-start.8) | async-done | bytes 1048608 | tf_op jit(solution)/shard_map/all_to_all | solution.py:69
  284.9 1.1 broadcast_in_dim.74
  286.0 3.7 all-to-all-start.7
  290.3 13.6 %all-to-all-done.7 = bf16[16,2,256,64]{2,3,1,0:T(8,128)(2,1)S(1)} async-done(((bf16[16,2,256,64]{2,3,1,0:T(8,128)(2,1)}), bf16[16,2,256,64]{2,3,1,0:T(8,128)(2,1)S(1)}, u32[]{:S(2)}, u32[]{:S(2)}) %all-to-all-start.7) | async-done | bytes 1048608 | tf_op jit(solution)/shard_map/all_to_all | solution.py:91
  303.9 3.3 all-to-all-start.9
  307.2 2.6 copy_bitcast_fusion.2
  309.8 5.4 %all-to-all-done.9 = f32[256,2,32]{0,2,1:T(8,128)S(1)} async-done(((f32[256,2,32]{0,2,1:T(8,128)}), f32[256,2,32]{0,2,1:T(8,128)S(1)}, u32[]{:S(2)}, u32[]{:S(2)}) %all-to-all-start.9) | async-done | bytes 65568 | tf_op jit(solution)/shard_map/all_to_all | solution.py:82
  315.2 3.6 all-to-all-start.1
  320.6 9.8 %all-to-all-done.1 = f32[96,16,128]{2,0,1:T(8,128)S(1)} async-done(((f32[96,16,128]{2,0,1:T(8,128)}), f32[96,16,128]{2,0,1:T(8,128)S(1)}, u32[]{:S(2)}, u32[]{:S(2)}) %all-to-all-start.1) | async-done | bytes 786464 | tf_op jit(solution)/shard_map/all_to_all | solution.py:69
  331.0 3.3 all-to-all-start.10
  335.1 7.2 %all-to-all-done.10 = bf16[2,2,256,32]{2,3,1,0:T(8,128)(2,1)S(1)} async-done(((bf16[2,2,256,32]{2,3,1,0:T(8,128)(2,1)}), bf16[2,2,256,32]{2,3,1,0:T(8,128)(2,1)S(1)}, u32[]{:S(2)}, u32[]{:S(2)}) %all-to-all-start.10) | async-done | bytes 65568 | tf_op jit(solution)/shard_map/all_to_all | solution.py:89
  342.3 3.3 all-to-all-start.2
  345.6 8.0 %all-to-all-done.2 = f32[96,2,64]{0,2,1:T(8,128)S(1)} async-done(((f32[96,2,64]{0,2,1:T(8,128)}), f32[96,2,64]{0,2,1:T(8,128)S(1)}, u32[]{:S(2)}, u32[]{:S(2)}) %all-to-all-start.2) | async-done | bytes 49184 | tf_op jit(solution)/shard_map/all_to_all | solution.py:82
  353.6 1.1 broadcast_in_dim.77
  354.7 3.7 all-to-all-start.11
  361.1 10.6 %all-to-all-done.11 = bf16[16,2,256,64]{2,3,1,0:T(8,128)(2,1)S(1)} async-done(((bf16[16,2,256,64]{2,3,1,0:T(8,128)(2,1)}), bf16[16,2,256,64]{2,3,1,0:T(8,128)(2,1)S(1)}, u32[]{:S(2)}, u32[]{:S(2)}) %all-to-all-start.11) | async-done | bytes 1048608 | tf_op jit(solution)/shard_map/all_to_all | solution.py:91
  372.3 3.3 all-to-all-start.3
  376.8 6.9 %all-to-all-done.3 = bf16[2,2,96,64]{2,3,1,0:T(8,128)(2,1)S(1)} async-done(((bf16[2,2,96,64]{2,3,1,0:T(8,128)(2,1)}), bf16[2,2,96,64]{2,3,1,0:T(8,128)(2,1)S(1)}, u32[]{:S(2)}, u32[]{:S(2)}) %all-to-all-start.3) | async-done | bytes 49184 | tf_op jit(solution)/shard_map/all_to_all | solution.py:89
  383.8 1.1 broadcast_in_dim.71
  384.8 3.6 all-to-all-start.4
  389.3 1.2 pad_maximum_fusion
  390.5 1.4 copy.111
  392.0 1.4 copy.112
  393.5 6.5 %all-to-all-done.4 = bf16[16,2,96,128]{3,2,1,0:T(8,128)(2,1)S(1)} async-done(((bf16[16,2,96,128]{3,2,1,0:T(8,128)(2,1)}), bf16[16,2,96,128]{3,2,1,0:T(8,128)(2,1)S(1)}, u32[]{:S(2)}, u32[]{:S(2)}) %all-to-all-start.4) | async-done | bytes 786464 | tf_op jit(solution)/shard_map/all_to_all | solution.py:91
  (105 shorter events, 25.4 us)
Async XLA Ops:
  7.2 351.2 %copy-start = (bf16[96,2048]{1,0:T(8,128)(2,1)S(1)}, bf16[96,2048]{1,0:T(8,128)(2,1)}, u32[]{:S(2)}) copy-start(bf16[96,2048]{1,0:T(8,128)(2,1)} %param.20) | copy-start | bytes 1179652
  7.2 3.2 copy-start.19
  7.2 3.2 copy-start.1
  7.2 74.3 %all-gather.3.cloned.1.call-start = ((), (), s32[]{:S(2)}) async-start(), calls=%async_computation.18 | async-start | bytes 12255232 | tf_op jit(solution)/shard_map/all_gather | solution.py:109
  10.3 144.5 %reduce-scatter.4.cloned.1.call-start = ((), (), s32[]{:S(2)}) async-start(), calls=%async_computation.15 | async-start | bytes 4718592 | tf_op jit(solution)/shard_map/reduce_scatter | solution.py:155
  11.6 74.8 %copy-start.10 = (bf16[256,768]{1,0:T(8,128)(2,1)}, bf16[256,768]{1,0:T(8,128)(2,1)S(1)}, u32[]{:S(2)}) copy-start(bf16[256,768]{1,0:T(8,128)(2,1)S(1)} %gather_fusion) | copy-start | bytes 1179652
  86.3 1.0 copy-start.12
  93.0 1.0 copy-start.20
  94.8 1.2 copy-start.13
  96.1 2.4 copy-start.14
  102.4 1.2 copy-start.4
  102.4 2.3 copy-start.11
  102.4 129.4 %reduce-scatter.6.cloned.1.call-start = ((), (), s32[]{:S(2)}) async-start(), calls=%async_computation.16 | async-start | bytes 4718592 | tf_op jit(solution)/shard_map/reduce_scatter | solution.py:170
  104.7 50.0 %copy-start.6 = (bf16[256,1024]{0,1:T(8,128)(2,1)}, bf16[256,1024]{0,1:T(8,128)(2,1)S(1)}, u32[]{:S(2)}) copy-start(bf16[256,1024]{0,1:T(8,128)(2,1)S(1)} %copy.118) | copy-start | bytes 1572868
  106.8 49.9 %copy-start.2 = (bf16[1,256,2048]{1,2,0:T(8,128)(2,1)}, bf16[1,256,2048]{1,2,0:T(8,128)(2,1)S(1)}, u32[]{:S(2)}) copy-start(bf16[1,256,2048]{1,2,0:T(8,128)(2,1)S(1)} %copy.93) | copy-start | bytes 3145732
  181.9 1.2 copy-start.15
  181.9 125.3 %reduce-scatter.8.cloned.1.call-start = ((), (), s32[]{:S(2)}) async-start(), calls=%async_computation.17 | async-start | bytes 3538944 | tf_op jit(solution)/shard_map/reduce_scatter | solution.py:179
  202.3 29.5 %copy-start.7 = (bf16[256,1024]{1,0:T(8,128)(2,1)S(1)}, bf16[256,1024]{1,0:T(8,128)(2,1)}, u32[]{:S(2)}) copy-start(bf16[256,1024]{1,0:T(8,128)(2,1)} %get-tuple-element.36) | copy-start | bytes 1572868
  231.8 21.9 %copy-start.3 = (bf16[1,256,2048]{1,2,0:T(8,128)(2,1)S(1)}, bf16[1,256,2048]{1,2,0:T(8,128)(2,1)}, u32[]{:S(2)}) copy-start(bf16[1,256,2048]{1,2,0:T(8,128)(2,1)} %copy-done.2) | copy-start | bytes 3145732
  232.1 24.5 %copy-start.5 = (bf16[256,1024]{0,1:T(8,128)(2,1)}, bf16[256,1024]{0,1:T(8,128)(2,1)S(1)}, u32[]{:S(2)}) copy-start(bf16[256,1024]{0,1:T(8,128)(2,1)S(1)} %copy.123) | copy-start | bytes 1572868
  234.4 13.8 %all-to-all-start.5 = ((f32[256,2,32]{0,2,1:T(8,128)}), f32[256,2,32]{0,2,1:T(8,128)}, u32[]{:S(2)}, u32[]{:S(2)}) async-start(f32[256,2,32]{0,2,1:T(8,128)} %bitcast.117), calls=%async_computation.8 | async-start | bytes 131072 | tf_op jit(solution)/shard_map/all_to_all | solution.py:82
  250.4 12.5 %all-to-all-start.6 = ((bf16[2,2,256,32]{2,3,1,0:T(8,128)(2,1)}), bf16[2,2,256,32]{2,3,1,0:T(8,128)(2,1)S(1)}, u32[]{:S(2)}, u32[]{:S(2)}) async-start(bf16[2,2,256,32]{2,3,1,0:T(8,128)(2,1)} %broadcast_in_dim.72), calls=%async_computation.9 | async-start | bytes 131072 | tf_op jit(solution)/shard_map/all_to_all | solution.py:89
  262.9 21.9 %all-to-all-start.8 = ((f32[256,16,64]{0,2,1:T(8,128)}), f32[256,16,64]{0,2,1:T(8,128)S(1)}, u32[]{:S(2)}, u32[]{:S(2)}) async-start(f32[256,16,64]{0,2,1:T(8,128)} %bitcast.34), calls=%async_computation.11 | async-start | bytes 2097152 | tf_op jit(solution)/shard_map/all_to_all | solution.py:69
  284.9 22.3 %copy-start.16 = (bf16[96,2048]{1,0:T(8,128)(2,1)S(1)}, bf16[96,2048]{1,0:T(8,128)(2,1)}, u32[]{:S(2)}) copy-start(bf16[96,2048]{1,0:T(8,128)(2,1)} %param.14) | copy-start | bytes 1179652
  284.9 22.4 %copy-start.17 = (bf16[1,96,2048]{2,1,0:T(8,128)(2,1)S(1)}, bf16[1,96,2048]{2,1,0:T(8,128)(2,1)}, u32[]{:S(2)}) copy-start(bf16[1,96,2048]{2,1,0:T(8,128)(2,1)} %param.18) | copy-start | bytes 1179652
  286.0 17.9 %all-to-all-start.7 = ((bf16[16,2,256,64]{2,3,1,0:T(8,128)(2,1)}), bf16[16,2,256,64]{2,3,1,0:T(8,128)(2,1)S(1)}, u32[]{:S(2)}, u32[]{:S(2)}) async-start(bf16[16,2,256,64]{2,3,1,0:T(8,128)(2,1)} %broadcast_in_dim.74), calls=%async_computation.10 | async-start | bytes 2097152 | tf_op jit(solution)/shard_map/all_to_all | solution.py:91
  303.9 11.3 %all-to-all-start.9 = ((f32[256,2,32]{0,2,1:T(8,128)}), f32[256,2,32]{0,2,1:T(8,128)S(1)}, u32[]{:S(2)}, u32[]{:S(2)}) async-start(f32[256,2,32]{0,2,1:T(8,128)} %bitcast.35), calls=%async_computation.12 | async-start | bytes 131072 | tf_op jit(solution)/shard_map/all_to_all | solution.py:82
  315.2 15.2 %all-to-all-start.1 = ((f32[96,16,128]{2,0,1:T(8,128)}), f32[96,16,128]{2,0,1:T(8,128)S(1)}, u32[]{:S(2)}, u32[]{:S(2)}) async-start(f32[96,16,128]{2,0,1:T(8,128)} %copy_bitcast_fusion.2), calls=%async_computation.4 | async-start | bytes 1572864 | tf_op jit(solution)/shard_map/all_to_all | solution.py:69
  331.0 11.3 %all-to-all-start.10 = ((bf16[2,2,256,32]{2,3,1,0:T(8,128)(2,1)}), bf16[2,2,256,32]{2,3,1,0:T(8,128)(2,1)S(1)}, u32[]{:S(2)}, u32[]{:S(2)}) async-start(bf16[2,2,256,32]{2,3,1,0:T(8,128)(2,1)} %broadcast_in_dim.75), calls=%async_computation.13 | async-start | bytes 131072 | tf_op jit(solution)/shard_map/all_to_all | solution.py:89
  342.3 11.3 %all-to-all-start.2 = ((f32[96,2,64]{0,2,1:T(8,128)}), f32[96,2,64]{0,2,1:T(8,128)S(1)}, u32[]{:S(2)}, u32[]{:S(2)}) async-start(f32[96,2,64]{0,2,1:T(8,128)} %bitcast.21), calls=%async_computation.5 | async-start | bytes 131072 | tf_op jit(solution)/shard_map/all_to_all | solution.py:82
  353.6 1.1 copy-start.18
  354.7 17.0 %all-to-all-start.11 = ((bf16[16,2,256,64]{2,3,1,0:T(8,128)(2,1)}), bf16[16,2,256,64]{2,3,1,0:T(8,128)(2,1)S(1)}, u32[]{:S(2)}, u32[]{:S(2)}) async-start(bf16[16,2,256,64]{2,3,1,0:T(8,128)(2,1)} %broadcast_in_dim.77), calls=%async_computation.14 | async-start | bytes 2097152 | tf_op jit(solution)/shard_map/all_to_all | solution.py:91
  372.3 11.3 %all-to-all-start.3 = ((bf16[2,2,96,64]{2,3,1,0:T(8,128)(2,1)}), bf16[2,2,96,64]{2,3,1,0:T(8,128)(2,1)S(1)}, u32[]{:S(2)}, u32[]{:S(2)}) async-start(bf16[2,2,96,64]{2,3,1,0:T(8,128)(2,1)} %broadcast_in_dim.69), calls=%async_computation.6 | async-start | bytes 131072 | tf_op jit(solution)/shard_map/all_to_all | solution.py:89
  384.8 15.2 %all-to-all-start.4 = ((bf16[16,2,96,128]{3,2,1,0:T(8,128)(2,1)}), bf16[16,2,96,128]{3,2,1,0:T(8,128)(2,1)S(1)}, u32[]{:S(2)}, u32[]{:S(2)}) async-start(bf16[16,2,96,128]{3,2,1,0:T(8,128)(2,1)} %broadcast_in_dim.71), calls=%async_computation.7 | async-start | bytes 1572864 | tf_op jit(solution)/shard_map/all_to_all | solution.py:91
  389.3 2.6 copy-start.8
  389.3 2.6 copy-start.9
Sparse Core Ops, SparseCore 0:
  10.4 71.0 all-gather.2
  102.5 52.1 reduce-scatter.3
  182.0 49.7 reduce-scatter.5
  234.2 46.0 reduce-scatter.7

commit v8 on v6

--- a/solution.py
+++ b/solution.py
@@ -62,16 +62,23 @@
     return embed_grad.astype(jnp.bfloat16)
 
 
-def wide_mean_update(delta, momentum, weights):
+def plane_sum(delta):
+    plane = ("y", "x")
+    n_plane = lax.axis_size(plane)
+    rows, cols = delta.shape
+    got = lax.all_to_all(delta, plane, 1, 0, tiled=True)
+    return jnp.sum(got.reshape(n_plane, rows, cols // n_plane), axis=0)
+
+
+def wide_mean_update(delta, momentum, weights, part=None):
     plane = ("y", "x")
     n_plane = lax.axis_size(plane)
     n_half = lax.axis_size("zh")
     sites = n_plane * n_half
-    rows, cols = delta.shape
+    rows, cols = momentum.shape
     p1 = cols // n_plane
     p2 = p1 // n_half
-    got = lax.all_to_all(delta, plane, 1, 0, tiled=True)
-    part = jnp.sum(got.reshape(n_plane, rows, p1), axis=0)
+    part = plane_sum(delta) if part is None else part
     got = lax.all_to_all(part, "zh", 1, 0, tiled=True)
     mean = jnp.sum(got.reshape(n_half, rows, p2), axis=0) / sites
     start = lax.axis_index(plane) * p1 + lax.axis_index("zh") * p2
@@ -157,13 +164,20 @@
     ).astype(jnp.bfloat16)
     term_first, grad_second = lax.optimization_barrier((term_first, grad_second))
     delta_second = adam_delta(grad_second, m_second[0], v_second[0], w_second)
-    new_second, vel_second = wide_mean_update(delta_second, mom_second, w_second)
+    part_second = plane_sum(delta_second)
     grad_first = lax.psum_scatter(
         term_first, NARROW, scatter_dimension=0, tiled=True
     ).astype(jnp.float32)
     delta_first = adam_delta(grad_first, m_first[0], v_first[0], w_first)
-    new_first, vel_first = wide_mean_update(delta_first, mom_first, w_first)
-    return (new_first, new_second, vel_first, vel_second)
+    part_first = plane_sum(delta_first)
+    rows_first = w_first.shape[0]
+    new_w, vel = wide_mean_update(
+        None,
+        jnp.concatenate([mom_first, mom_second], axis=0),
+        jnp.concatenate([w_first, w_second], axis=0),
+        jnp.concatenate([part_first, part_second], axis=0),
+    )
+    return (new_w[:rows_first], new_w[rows_first:], vel[:rows_first], vel[rows_first:])
 
 
 def solution(mesh):

time: 368 us -> 357 us (0.970)
  waiting for transfers between devices: 212 us -> 195 us
  blocking collectives: 36.2 us -> 50.2 us
  starting transfers between devices: 26.5 us -> 17.1 us
    all_to_all x5 -> x2, waiting for transfers between devices: 55.6 us -> 17 us  [plane_sum(): got = lax.all_to_all(delta, plane, 1, 0, tiled=True)]
    reduce_scatter x1, waiting for transfers between devices: 0.01 us -> 31.8 us  [shards(): lax.psum_scatter(term_first, NARROW, scatter_dimension=0, tiled=True)]
    all_to_all x1 -> x2, blocking collectives: 36.2 us -> 50.2 us  [the longest x1 38.9 us: wide_mean_update(): lax.all_to_all(jnp.broadcast_to(back[None], (n_plane,) + back.shape), pla...]
    all_to_all x2 -> x1, waiting for transfers between devices: 13.8 us -> 4.41 us  [wide_mean_update(): got = lax.all_to_all(part, 'zh', 1, 0, tiled=True)]
    unnamed x28 -> x30, local copies, waits for them, and re-layouts: 6.15 us -> 12.1 us
    all_to_all x5 -> x2, starting transfers between devices: 18.3 us -> 13.4 us  [plane_sum(): got = lax.all_to_all(delta, plane, 1, 0, tiled=True)]
    all_to_all x2 -> x1, starting transfers between devices: 7.93 us -> 3.43 us  [wide_mean_update(): got = lax.all_to_all(part, 'zh', 1, 0, tiled=True)]
  transfers between devices with their start and end apart: 10 -> 6, of which waited for: 9 -> 6; matrix products, arithmetic and copies ran while one was open for 11% -> 9% of each run, Pallas kernels for 0% -> 0%
where the time goes in v8:
time: 357 us; the launch traced here: 354 us
  waiting for transfers between devices  195 us (55%)
  blocking collectives  50.2 us (14%)
  local copies, waits for them, and re-layouts  34.6 us (10%)
  matrix products  30.3 us (8%)
  starting transfers between devices  17.1 us (5%)
  between operations  14.1 us (4%)
  other arithmetic  12.7 us (4%)
    reduce_scatter x1, waiting for transfers between devices, shards(): lax.psum_scatter((scale_two * jnp.dot(active.T, embed_half, preferred_ele...  72.3 us
    all_gather x1, waiting for transfers between devices, gather_weights(): got = lax.all_gather(mine, ('zh',) + NARROW, axis=0, tiled=False)  69.8 us
    all_to_all x1, blocking collectives, wide_mean_update(): lax.all_to_all(jnp.broadcast_to(back[None], (n_plane,) + back.shape), pla...  38.9 us
    reduce_scatter x1, waiting for transfers between devices, shards(): lax.psum_scatter(term_first, NARROW, scatter_dimension=0, tiled=True)  31.8 us
    all_to_all x2, waiting for transfers between devices, plane_sum(): got = lax.all_to_all(delta, plane, 1, 0, tiled=True)  17 us
    all_to_all x2, starting transfers between devices, plane_sum(): got = lax.all_to_all(delta, plane, 1, 0, tiled=True)  13.4 us
    unnamed x30, local copies, waits for them, and re-layouts  12.1 us
    all_to_all x1, blocking collectives, wide_mean_update(): lax.all_to_all(jnp.broadcast_to(both[None], (n_half,) + both.shape), 'zh'...  11.3 us
  transfers between devices with their start and end apart: 6, of which 6 were waited for; matrix products, arithmetic and copies ran while one was open for 9% of the time, Pallas kernels for 0%

profile of v8, /device:TPU:64, one launch (start us, length us, event | category | flops | bytes accessed | tf_op | source)
XLA Modules:
  0.0 354.3 jit_solution(15545826880929783917)
XLA Ops:
  7.2 1.1 constant_dynamic-slice_fusion
  8.3 0.9 constant_dynamic-slice_fusion.1
  9.3 0.9 pad_maximum_fusion
  10.3 1.2 gather_fusion
  11.7 69.8 %all-gather.3.cloned.1.call-done = bf16[2816,2048]{1,0:T(8,128)(2,1)} async-done(((bf16[176,2048]{1,0:T(8,128)(2,1)}), bf16[2816,2048]{1,0:T(8,128)(2,1)}) %all-gather.3.cloned.1.call-update) | async-done | bytes 11534352 | tf_op jit(solution)/shard_map/all_gather | solution.py:109
  81.5 4.8 %multiply_convert_fusion.3 = (bf16[256,2048]{1,0:T(8,128)(2,1)S(1)}, f32[256,2048]{1,0:T(8,128)}) fusion(bf16[2,8,176,2048]{3,2,1,0:T(8,128)(2,1)} %bitcast.96, bf16[256,8,2,48]{0,3,2,1:T(8,128)(2,1)S(1)} %bitcast.93, pred[256]{0:T(512)(128)(4,1)S(1)} %compare_and_fusion), kind=kOutput, calls=%fused_computation.35 | convolution fusion | flops 810745856 | bytes 6684928 | tf_op jit(solution)/shard_map/bnhr,hnrc->bc/dot_general | solution.py:138
  86.3 1.0 copy-done.6
  87.3 1.5 reshape.106
  88.8 5.2 %multiply_reduce_fusion.1 = (f32[256]{0:T(256)S(1)}, f32[256,2048]{1,0:T(8,128)S(1)}) fusion(bf16[2,8,176,2048]{3,2,1,0:T(8,128)(2,1)} %bitcast.97, bf16[256,8,2,128]{3,2,1,0:T(2,128)(2,1)} %reshape.106), kind=kOutput, calls=%fused_computation.34 | convolution fusion | flops 2149056256 | bytes 11535360 | tf_op jit(solution)/shard_map/bnhr,hnrc->bc/dot_general | solution.py:145
  94.1 0.6 convolution_multiply_fusion.1
  95.1 0.8 multiply_reduce_fusion
  95.9 0.5 multiply_convert_fusion.2
  96.4 1.0 copy-done.8
  97.4 5.7 %multiply_convert_fusion = bf16[2048,2048]{1,0:T(8,128)(2,1)} fusion(bf16[256,2048]{1,0:T(8,128)(2,1)S(1)} %copy-done.7, bf16[256,2048]{1,0:T(8,128)(2,1)S(1)} %multiply_convert_fusion.2), kind=kOutput, calls=%fused_computation.1 | convolution fusion | flops 2155872256 | bytes 10485760 | tf_op jit(solution)/shard_map/dot_general | solution.py:151
  103.3 1.0 copy-done.9
  104.3 7.1 %multiply_bitcast_fusion = f32[256,8,2,128]{0,3,1,2:T(8,128)} fusion(bf16[2,8,176,2048]{3,2,1,0:T(8,128)(2,1)} %bitcast.98, bf16[256,2048]{1,0:T(8,128)(2,1)S(1)} %copy-done.9), kind=kOutput, calls=%fused_computation.31 | convolution fusion | flops 2148007936 | bytes 11534336 | tf_op jit(solution)/shard_map/bc,hnrc->bnhr/dot_general | solution.py:158
  111.4 3.2 copy.48
  114.6 2.7 mul.261
  117.3 6.1 %multiply_convert_fusion.1 = bf16[768,2048]{1,0:T(8,128)(2,1)} fusion(f32[256,2048]{1,0:T(8,128)} %get-tuple-element.21, f32[256,2048]{1,0:T(8,128)} %mul.261, bf16[256,768]{1,0:T(8,128)(2,1)S(1)} %gather_fusion, pred[256]{0:T(512)(128)(4,1)S(1)} %compare_and_fusion), kind=kOutput, calls=%fused_computation.6 | convolution fusion | flops 819134464 | bytes 7733504 | tf_op jit(solution)/shard_map/dot_general | solution.py:163
  123.4 72.3 %reduce-scatter.3.cloned.1.call-done = bf16[256,2048]{1,0:T(8,128)(2,1)} async-done(((bf16[2048,2048]{1,0:T(8,128)(2,1)}), bf16[256,2048]{1,0:T(8,128)(2,1)}) %reduce-scatter.3.cloned.1.call-update) | async-done | bytes 1048592 | tf_op jit(solution)/shard_map/reduce_scatter | solution.py:150
  195.7 1.5 convert_element_type.78
  197.2 1.2 copy-done.2
  198.4 4.5 %copy_bitcast_fusion = f32[256,16,128]{2,0,1:T(8,128)} fusion(bf16[256,2048]{1,0:T(8,128)(2,1)S(1)} %copy-done.2, f32[256,2048]{1,0:T(8,128)S(1)} %convert_element_type.78, bf16[1,256,2048]{2,1,0:T(8,128)(2,1)} %param.19, bf16[1,256,2048]{2,1,0:T(8,128)(2,1)} %param.17), kind=kLoop, calls=%fused_computation.29 | loop fusion | flops 7864320 | bytes 7340032 | tf_op jit(solution)/shard_map/all_to_all | solution.py:69
  202.9 6.8 %all-to-all-start.1 = ((f32[256,16,128]{2,0,1:T(8,128)}), f32[256,16,128]{2,0,1:T(8,128)S(1)}, u32[]{:S(2)}, u32[]{:S(2)}) async-start(f32[256,16,128]{2,0,1:T(8,128)} %copy_bitcast_fusion), calls=%async_computation.3 | async-start | bytes 4194304 | tf_op jit(solution)/shard_map/all_to_all | solution.py:69
  209.7 31.8 %reduce-scatter.5.cloned.1.call-done = bf16[96,2048]{1,0:T(8,128)(2,1)} async-done(((bf16[768,2048]{1,0:T(8,128)(2,1)}), bf16[96,2048]{1,0:T(8,128)(2,1)}) %reduce-scatter.5.cloned.1.call-update) | async-done | bytes 393232 | tf_op jit(solution)/shard_map/reduce_scatter | solution.py:168
  241.5 2.8 copy_bitcast_fusion.1
  244.3 0.3 all-to-all-done.1
  244.6 6.6 %all-to-all-start = ((f32[96,16,128]{2,0,1:T(8,128)}), f32[96,16,128]{2,0,1:T(8,128)}, u32[]{:S(2)}, u32[]{:S(2)}) async-start(f32[96,16,128]{2,0,1:T(8,128)} %copy_bitcast_fusion.1), calls=%async_computation.2 | async-start | bytes 1572864 | tf_op jit(solution)/shard_map/all_to_all | solution.py:69
  251.3 16.7 %all-to-all-done = f32[96,16,128]{2,0,1:T(8,128)} async-done(((f32[96,16,128]{2,0,1:T(8,128)}), f32[96,16,128]{2,0,1:T(8,128)}, u32[]{:S(2)}, u32[]{:S(2)}) %all-to-all-start) | async-done | bytes 786464 | tf_op jit(solution)/shard_map/all_to_all | solution.py:69
  268.0 1.2 reduce_sum.57
  269.2 0.8 copy.53
  270.0 3.4 all-to-all-start.2
  273.5 0.5 copy.43
  274.0 0.3 copy.42
  274.3 1.5 copy.55
  275.8 2.0 copy.54
  277.8 4.4 %all-to-all-done.2 = f32[352,2,64]{0,2,1:T(8,128)S(1)} async-done(((f32[352,2,64]{0,2,1:T(8,128)}), f32[352,2,64]{0,2,1:T(8,128)S(1)}, u32[]{:S(2)}, u32[]{:S(2)}) %all-to-all-start.2) | async-done | bytes 180256 | tf_op jit(solution)/shard_map/all_to_all | solution.py:82
  282.2 0.8 fusion.67
  283.2 11.3 %all_to_all.49 = bf16[2,2,352,64]{2,3,1,0:T(8,128)(2,1)S(1)} all-to-all(bf16[2,2,352,64]{2,3,1,0:T(8,128)(2,1)S(1)} %broadcast_in_dim.43), channel_id=1, replica_groups=mesh['zh'=2,'y'=4,'x'=4,'zl'=4,'c'=2] {'zh'}, dimensions={0} | all-to-all | bytes 360448 | tf_op jit(solution)/shard_map/all_to_all | solution.py:89
  294.6 0.6 broadcast_in_dim.45
  295.2 38.9 %all_to_all.50 = bf16[16,2,352,128]{3,2,1,0:T(8,128)(2,1)} all-to-all(bf16[16,2,352,128]{3,2,1,0:T(8,128)(2,1)S(1)} %broadcast_in_dim.45), channel_id=1, replica_groups=mesh['zh'=2,'y'=4,'x'=4,'zl'=4,'c'=2] {'y','x'}, dimensions={0} | all-to-all | bytes 5767168 | tf_op jit(solution)/shard_map/all_to_all | solution.py:91
  334.1 3.4 copy.58
  337.5 1.2 fusion.78
  338.6 2.3 fusion.77
  341.0 2.1 copy.66
  343.1 2.3 copy.61
  345.4 1.0 copy.67
  346.3 1.4 copy.62
  (42 shorter events, 1.4 us)
Async XLA Ops:
  7.2 3.1 copy-start
  7.2 3.1 copy-start.10
  7.2 74.3 %all-gather.3.cloned.1.call-start = ((), (), s32[]{:S(2)}) async-start(), calls=%async_computation.9 | async-start | bytes 12255232 | tf_op jit(solution)/shard_map/all_gather | solution.py:109
  10.2 185.5 %reduce-scatter.3.cloned.1.call-start = ((), (), s32[]{:S(2)}) async-start(), calls=%async_computation.7 | async-start | bytes 9437184 | tf_op jit(solution)/shard_map/reduce_scatter | solution.py:150
  86.3 1.0 copy-start.6
  94.1 1.0 copy-start.11
  95.9 1.5 copy-start.7
  96.4 1.0 copy-start.8
  103.1 1.2 copy-start.9
  103.1 138.4 %reduce-scatter.5.cloned.1.call-start = ((), (), s32[]{:S(2)}) async-start(), calls=%async_computation.8 | async-start | bytes 3538944 | tf_op jit(solution)/shard_map/reduce_scatter | solution.py:168
  197.2 1.2 copy-start.2
  202.9 41.7 %all-to-all-start.1 = ((f32[256,16,128]{2,0,1:T(8,128)}), f32[256,16,128]{2,0,1:T(8,128)S(1)}, u32[]{:S(2)}, u32[]{:S(2)}) async-start(f32[256,16,128]{2,0,1:T(8,128)} %copy_bitcast_fusion), calls=%async_computation.3 | async-start | bytes 4194304 | tf_op jit(solution)/shard_map/all_to_all | solution.py:69
  244.6 23.4 %all-to-all-start = ((f32[96,16,128]{2,0,1:T(8,128)}), f32[96,16,128]{2,0,1:T(8,128)}, u32[]{:S(2)}, u32[]{:S(2)}) async-start(f32[96,16,128]{2,0,1:T(8,128)} %copy_bitcast_fusion.1), calls=%async_computation.2 | async-start | bytes 1572864 | tf_op jit(solution)/shard_map/all_to_all | solution.py:69
  251.3 22.7 %copy-start.4 = (bf16[96,2048]{1,0:T(8,128)(2,1)S(1)}, bf16[96,2048]{1,0:T(8,128)(2,1)}, u32[]{:S(2)}) copy-start(bf16[96,2048]{1,0:T(8,128)(2,1)} %param.14) | copy-start | bytes 1179652
  270.0 12.2 %all-to-all-start.2 = ((f32[352,2,64]{0,2,1:T(8,128)}), f32[352,2,64]{0,2,1:T(8,128)S(1)}, u32[]{:S(2)}, u32[]{:S(2)}) async-start(f32[352,2,64]{0,2,1:T(8,128)} %bitcast.20), calls=%async_computation.4 | async-start | bytes 393216 | tf_op jit(solution)/shard_map/all_to_all | solution.py:82
  341.0 4.4 %copy-start.5 = (bf16[1,96,16,128]{1,3,2,0:T(8,128)(2,1)S(1)}, bf16[1,96,16,128]{1,3,2,0:T(8,128)(2,1)}, u32[]{:S(2)}) copy-start(bf16[1,96,16,128]{1,3,2,0:T(8,128)(2,1)} %get-tuple-element.16) | copy-start | bytes 1179652
  341.0 5.4 %copy-start.3 = (bf16[1,256,16,128]{1,3,2,0:T(8,128)(2,1)S(1)}, bf16[1,256,16,128]{1,3,2,0:T(8,128)(2,1)}, u32[]{:S(2)}) copy-start(bf16[1,256,16,128]{1,3,2,0:T(8,128)(2,1)} %get-tuple-element.14) | copy-start | bytes 3145732
  343.1 4.7 %copy-start.1 = (bf16[1,128,768]{2,1,0:T(8,128)(2,1)S(1)}, bf16[1,128,768]{2,1,0:T(8,128)(2,1)}, u32[]{:S(2)}) copy-start(bf16[1,128,768]{2,1,0:T(8,128)(2,1)} %param.11) | copy-start | bytes 589828
Sparse Core Ops, SparseCore 0:
  10.4 71.0 all-gather.2
  103.2 92.4 reduce-scatter.2
  198.3 43.1 reduce-scatter.4
